TPU v7x, 32 devices: a whole 2x2x4 slice. The times are simulated.
32 devices in a mesh: grp: 2 (over x), gx: 8 (over z, y), gy: 2 (over core).
Axes of the slice: x: 2, y: 2, z: 4, core: 2. Of those that a mesh axis runs over, the one named last changes fastest.
Arguments:
- spectrum: float32 [16, 96, 1152], P('gx', 'gy', 'grp'), may hold values from 0 to 2
- wet_mask: int32 [16, 96], P('gx', 'gy'), may hold values 0 or 1
- ocean_source: int32 [16, 96], P('gx', 'gy'), may hold values from 0 to 95
- ocean_u: float32 [16, 96, 40], P('gx', 'gy', 'grp'), may hold values from -2 to 2
- ocean_v: float32 [16, 96, 40], P('gx', 'gy', 'grp'), may hold values from -2 to 2
- current_weights: float32 [40, 32], replicated, may hold values from 0.005 to 0.04
- drift_weights: float32 [40, 32], replicated, may hold values from 0.005 to 0.05
- inter_left: bfloat16 [1152, 512], P('grp'), may hold values from -0.25 to 0.25
- inter_right: bfloat16 [1152, 512], P('grp'), may hold values from -0.25 to 0.25
- inter_out: bfloat16 [512, 1152], P(None, 'grp'), may hold values from -0.25 to 0.25
- mixing: float32 [40, 40], P(None, 'grp'), may hold values from -0.47434166 to 0.47434166
Outputs:
- spectrum_out: float32 [16, 96, 1152], P('gx', 'gy', 'grp')
- ocean_u_out: float32 [16, 96, 40], P('gx', 'gy', 'grp')
- ocean_v_out: float32 [16, 96, 40], P('gx', 'gy', 'grp')
- drift_u: float32 [16, 96, 40], P('gx', 'gy', 'grp')
- drift_v: float32 [16, 96, 40], P('gx', 'gy', 'grp')
Inputs may be any that keep to these rules, and one draw needn't show every extreme that they name: `wet_mask`: 1 marks a sea column, 0 a land column. `ocean_source`: each entry numbers a column of the same tile of 2 x 48 columns as (x mod 2) * 48 + (y mod 48).
All inputs are finite; a program needn't handle non-finite values. No bound on the sum of `wet_mask` on one device may be relied on, other than what follows from the above.
Results may differ from a plain program's by a relative error of at most 0.00077.
Values sent between devices are 32-bit elements; how exact they have to be, the bound alone decides.
A program may use at most 64 MiB of HBM per device.

v0:
```python
import jax
import jax.numpy as jnp
from jax import lax
from jax.sharding import PartitionSpec as P

NF = 32
ND = 36
NLEV = 40
WAVE_SECTIONS = 3
OCEAN_SECTIONS = 2
NFL = 16


highest = lax.Precision.HIGHEST
inter_step = 0.1
ocean_step = 0.4
coriolis = 0.5
viscosity = 0.1


def extended(array, sides, width):
    for axis, dim in sides:
        size, length = (lax.axis_size(axis), array.shape[dim])
        up = [(i, (i + 1) % size) for i in range(size - 1)]
        down = [(j, i) for i, j in up]
        last = lax.slice_in_dim(array, length - width, length, axis=dim)
        leading = lax.slice_in_dim(array, 0, width, axis=dim)
        before = lax.ppermute(last, axis, up)
        after = lax.ppermute(leading, axis, down)
        array = jnp.concatenate([before, array, after], axis=dim)
    return array


def bin_tables(band_index, bin_count):
    position = jnp.arange(bin_count)
    direction = (position // NFL).astype(jnp.float32)
    frequency = (band_index * NFL + position % NFL).astype(jnp.float32)
    angle_value = 2.0 * jnp.pi * direction / ND
    group_speed = 0.2 + 0.4 * (NF - 1 - frequency) / (NF - 1)
    turning = 0.5 * (frequency + 1.0) / NF
    return (jnp.cos(angle_value), jnp.sin(angle_value), group_speed, turning)


def beam_sweep(padded, velocity, which_axis):
    extent = velocity.shape[which_axis]

    def take_part(offset):
        return lax.slice_in_dim(padded, offset, offset + extent, axis=which_axis)

    centre = take_part(2)
    upwind_one = jnp.where(velocity >= 0.0, take_part(1), take_part(3))
    beyond = jnp.where(velocity >= 0.0, take_part(0), take_part(4))
    magnitude = jnp.abs(velocity)
    return (
        centre
        - 0.5 * magnitude * (3.0 * centre - 4.0 * upwind_one + beyond)
        + 0.5 * magnitude * magnitude * (centre - 2.0 * upwind_one + beyond)
    )


def body(
    spectrum,
    wet_mask,
    ocean_source,
    ocean_u,
    ocean_v,
    current_weights,
    drift_weights,
    inter_left,
    inter_right,
    inter_out,
    mixing,
):
    band_index = lax.axis_index("grp")
    tile_x = spectrum.shape[0]
    tile_y = spectrum.shape[1]
    bin_count = spectrum.shape[2]
    levels_own = ocean_u.shape[2]
    cosine, sine_value, group_speed, turning = bin_tables(band_index, bin_count)
    wet_factor = wet_mask.astype(jnp.float32)[:, :, None]
    flat_source = ocean_source.reshape(-1)
    whole_u, whole_v = (
        lax.all_gather(ocean_u, "grp", axis=2, tiled=True),
        lax.all_gather(ocean_v, "grp", axis=2, tiled=True),
    )
    weights_band = lax.dynamic_slice_in_dim(current_weights, band_index * NFL, NFL, 1)
    picked_u = jnp.take(whole_u.reshape(tile_x * tile_y, NLEV), flat_source, axis=0)
    picked_v = jnp.take(whole_v.reshape(tile_x * tile_y, NLEV), flat_source, axis=0)
    flow_x = jnp.dot(picked_u, weights_band, precision=highest, preferred_element_type=jnp.float32)
    flow_y = jnp.dot(picked_v, weights_band, precision=highest, preferred_element_type=jnp.float32)
    flow_x = flow_x.reshape(tile_x, tile_y, NFL)
    flow_y = flow_y.reshape(tile_x, tile_y, NFL)
    flow_x_bins = jnp.tile(flow_x, (1, 1, ND))
    flow_y_bins = jnp.tile(flow_y, (1, 1, ND))
    speed_y = group_speed * sine_value + flow_y_bins
    turn_rate = turning * (sine_value * flow_x_bins - cosine * flow_y_bins)
    current_pad = extended(jnp.concatenate([flow_x, flow_y], axis=2), (("gx", 0), ("gy", 1)), 2)
    speed_x_wide = group_speed * cosine + jnp.tile(current_pad[2 : tile_x + 2, :, :NFL], (1, 1, ND))
    spectrum_now = wet_factor * spectrum
    for repeat in range(WAVE_SECTIONS):
        padded = extended(spectrum_now, (("gx", 0), ("gy", 1)), 2)
        shifted = beam_sweep(padded, speed_x_wide, 0)
        shifted = beam_sweep(shifted, speed_y, 1)
        behind = jnp.roll(shifted, NFL, axis=2)
        ahead_dir = jnp.roll(shifted, -NFL, axis=2)
        upwind = jnp.where(turn_rate >= 0.0, behind, ahead_dir)
        turned = shifted - jnp.abs(turn_rate) * (shifted - upwind)
        flat_bins = spectrum_now.reshape(-1, bin_count).astype(jnp.bfloat16)
        product = jnp.dot(flat_bins, inter_left, preferred_element_type=jnp.float32) * jnp.dot(
            flat_bins, inter_right, preferred_element_type=jnp.float32
        )
        source = inter_step * jnp.dot(
            product.astype(jnp.bfloat16), inter_out, preferred_element_type=jnp.float32
        )
        spectrum_now = wet_factor * (turned + source.reshape(spectrum_now.shape))
    profile = jnp.tile(lax.dynamic_slice_in_dim(drift_weights, band_index * NFL, NFL, 1), (1, ND))
    final_flat = spectrum_now.reshape(-1, bin_count)
    contract = (((1,), (1,)), ((), ()))
    part_x = lax.dot_general(
        final_flat,
        profile * cosine,
        contract,
        precision=highest,
        preferred_element_type=jnp.float32,
    )
    part_y = lax.dot_general(
        final_flat,
        profile * sine_value,
        contract,
        precision=highest,
        preferred_element_type=jnp.float32,
    )
    drift_x, drift_y = (
        lax.psum_scatter(part_x, "grp", scatter_dimension=1, tiled=True),
        lax.psum_scatter(part_y, "grp", scatter_dimension=1, tiled=True),
    )
    drift_x = drift_x.reshape(tile_x, tile_y, levels_own)
    drift_y = drift_y.reshape(tile_x, tile_y, levels_own)
    velocity_u = ocean_u
    velocity_v = ocean_v
    for repeat in range(OCEAN_SECTIONS):
        stacked = jnp.concatenate([velocity_u, velocity_v], axis=2)
        padded = extended(stacked, (("gx", 0), ("gy", 1)), 1)
        laplace_both = (
            padded[2:, 1:-1]
            + padded[:-2, 1:-1]
            + padded[1:-1, 2:]
            + padded[1:-1, :-2]
            - 4.0 * stacked
        )
        laplace_u = laplace_both[:, :, :levels_own]
        laplace_v = laplace_both[:, :, levels_own:]
        first_u = velocity_u + ocean_step * (
            coriolis * (velocity_v + drift_y) + viscosity * laplace_u
        )
        first_v = velocity_v + ocean_step * (
            -coriolis * (velocity_u + drift_x) + viscosity * laplace_v
        )
        whole_u, whole_v = (
            lax.all_gather(first_u, "grp", axis=2, tiled=True),
            lax.all_gather(first_v, "grp", axis=2, tiled=True),
        )
        velocity_u = wet_factor * (
            first_u + jnp.einsum("abk,kl->abl", whole_u, mixing, precision=highest)
        )
        velocity_v = wet_factor * (
            first_v + jnp.einsum("abk,kl->abl", whole_v, mixing, precision=highest)
        )
    return (spectrum_now, velocity_u, velocity_v, drift_x, drift_y)


def solution(mesh):
    in_specs = (
        P("gx", "gy", "grp"),
        P("gx", "gy"),
        P("gx", "gy"),
        P("gx", "gy", "grp"),
        P("gx", "gy", "grp"),
        P(),
        P(),
        P("grp", None),
        P("grp", None),
        P(None, "grp"),
        P(None, "grp"),
    )
    out_specs = (
        P("gx", "gy", "grp"),
        P("gx", "gy", "grp"),
        P("gx", "gy", "grp"),
        P("gx", "gy", "grp"),
        P("gx", "gy", "grp"),
    )
    return jax.shard_map(body, mesh=mesh, in_specs=in_specs, out_specs=out_specs, check_vma=False)
```

profile of v0, /device:TPU:24, one launch (start us, length us, event | category | flops | bytes accessed | tf_op | source)
XLA Modules:
  0.0 159.7 jit_solution(4556036495489061007)
XLA Ops:
  0.7 0.7 copy-done.29
  1.5 4.5 %all_gather.18 = f32[2,48,40]{1,0,2:T(2,128)S(1)} all-gather(f32[2,48,20]{1,0,2:T(2,128)S(1)} %copy-done.17), channel_id=1, replica_groups=mesh['grp'=2,'gx'=8,'gy'=2] {'grp'}, dimensions={2}, use_global_device_ids=true | all-gather | bytes 23040 | tf_op jit(solution)/shard_map/all_gather | solution.py:83
  7.1 0.7 copy-done.18
  7.8 4.4 %all_gather.19 = f32[2,48,40]{1,0,2:T(2,128)S(1)} all-gather(f32[2,48,20]{1,0,2:T(2,128)S(1)} %copy-done.18), channel_id=1, replica_groups=mesh['grp'=2,'gx'=8,'gy'=2] {'grp'}, dimensions={2}, use_global_device_ids=true | all-gather | bytes 23040 | tf_op jit(solution)/shard_map/all_gather | solution.py:84
  13.4 3.4 %collective-permute-start.4 = (f32[2,48,32]{1,0,2:T(2,128)S(1)}, f32[2,48,32]{1,0,2:T(2,128)}, u32[]{:S(2)}, u32[]{:S(2)}) collective-permute-start(f32[2,48,32]{1,0,2:T(2,128)S(1)} %constant_dynamic-update-slice_fusion), channel_id=1, source_target_pairs={{0,2},{2,4},{4,6},{6,8},{8,10},{10,12},{12,14},{1,3},{3,5},{5,7},{... | collective-permute-start | bytes 36872 | tf_op jit(solution)/shard_map/ppermute | solution.py:28
  16.8 3.3 %collective-permute-start.5 = (f32[2,48,32]{1,0,2:T(2,128)S(1)}, f32[2,48,32]{1,0,2:T(2,128)}, u32[]{:S(2)}, u32[]{:S(2)}) collective-permute-start(f32[2,48,32]{1,0,2:T(2,128)S(1)} %constant_dynamic-update-slice_fusion), channel_id=1, source_target_pairs={{2,0},{4,2},{6,4},{8,6},{10,8},{12,10},{14,12},{3,1},{5,3},{7,5},{... | collective-permute-start | bytes 36872 | tf_op jit(solution)/shard_map/ppermute | solution.py:29
  20.7 3.2 %collective-permute-start = (f32[2,48,576]{2,1,0:T(8,128)S(1)}, f32[2,48,576]{2,1,0:T(8,128)S(1)}, u32[]{:S(2)}, u32[]{:S(2)}) collective-permute-start(f32[2,48,576]{2,1,0:T(8,128)S(1)} %get-tuple-element.49), channel_id=1, source_target_pairs={{0,2},{2,4},{4,6},{6,8},{8,10},{10,12},{12,14},{1,3},{3,5},{5,7},{... | collective-permute-start | bytes 663560 | tf_op jit(solution)/shard_map/ppermute | solution.py:28
  24.6 3.6 %collective-permute-start.16 = (f32[1,48,40]{1,2,0:T(8,128)}, f32[1,48,40]{1,2,0:T(8,128)}, u32[]{:S(2)}, u32[]{:S(2)}) collective-permute-start(f32[1,48,40]{1,2,0:T(8,128)} %get-tuple-element.81), channel_id=1, source_target_pairs={{2,0},{4,2},{6,4},{8,6},{10,8},{12,10},{14,12},{3,1},{5,3},{7,5},{... | collective-permute-start | bytes 23048 | tf_op jit(solution)/shard_map/ppermute | solution.py:29
  28.2 2.8 %collective-permute-start.17 = (f32[1,48,40]{1,2,0:T(8,128)}, f32[1,48,40]{1,2,0:T(8,128)}, u32[]{:S(2)}, u32[]{:S(2)}) collective-permute-start(f32[1,48,40]{1,2,0:T(8,128)} %get-tuple-element.80), channel_id=1, source_target_pairs={{0,2},{2,4},{4,6},{6,8},{8,10},{10,12},{12,14},{1,3},{3,5},{5,7},{... | collective-permute-start | bytes 23048 | tf_op jit(solution)/shard_map/ppermute | solution.py:28
  31.0 0.6 fusion.98
  31.6 0.6 fusion.92
  32.7 1.2 convolution_multiply_fusion.2
  33.9 0.9 broadcast_multiply_fusion
  35.7 0.8 pad_maximum_fusion.4
  36.4 0.7 fusion.117
  37.1 1.3 collective-permute-start.18
  38.4 4.3 %collective-permute-start.19 = (f32[4,1,40]{1,2,0:T(8,128)}, f32[4,1,40]{1,2,0:T(8,128)}, u32[]{:S(2)}, u32[]{:S(2)}) collective-permute-start(f32[4,1,40]{1,2,0:T(8,128)} %get-tuple-element.77), channel_id=1, source_target_pairs={{0,1},{2,3},{4,5},{6,7},{8,9},{10,11},{12,13},{14,15},{16,17},{18,... | collective-permute-start | bytes 1928 | tf_op jit(solution)/shard_map/ppermute | solution.py:28
  42.7 0.9 copy.297
  43.6 0.7 copy-done.30
  45.5 4.0 %collective-permute-start.1 = (f32[2,48,576]{2,1,0:T(8,128)S(1)}, f32[2,48,576]{2,1,0:T(8,128)S(1)}, u32[]{:S(2)}, u32[]{:S(2)}) collective-permute-start(f32[2,48,576]{2,1,0:T(8,128)S(1)} %get-tuple-element.49), channel_id=1, source_target_pairs={{2,0},{4,2},{6,4},{8,6},{10,8},{12,10},{14,12},{3,1},{5,3},{7,5},{... | collective-permute-start | bytes 663560 | tf_op jit(solution)/shard_map/ppermute | solution.py:29
  49.5 0.9 fusion.41
  50.5 0.8 pad_maximum_fusion.3
  51.4 1.3 collective-permute-start.6
  52.7 1.3 collective-permute-start.7
  54.1 0.7 pad_maximum_fusion.40
  54.9 3.6 %collective-permute-start.2 = (f32[6,2,576]{2,1,0:T(2,128)}, f32[6,2,576]{2,1,0:T(2,128)}, u32[]{:S(2)}, u32[]{:S(2)}) collective-permute-start(f32[6,2,576]{2,1,0:T(2,128)} %get-tuple-element.54), channel_id=1, source_target_pairs={{0,1},{2,3},{4,5},{6,7},{8,9},{10,11},{12,13},{14,15},{16,17},{18,... | collective-permute-start | bytes 82952 | tf_op jit(solution)/shard_map/ppermute | solution.py:28
  58.5 1.3 collective-permute-start.3
  59.8 0.9 pad_maximum_fusion.41
  61.0 0.9 collective-permute-done.3
  61.9 1.2 pad_maximum_fusion
  64.3 0.7 copy-done.11
  65.3 1.9 %collective-permute-start.8 = (f32[2,48,576]{2,1,0:T(8,128)S(1)}, f32[2,48,576]{2,1,0:T(8,128)S(1)}, u32[]{:S(2)}, u32[]{:S(2)}) collective-permute-start(f32[2,48,576]{2,1,0:T(8,128)S(1)} %get-tuple-element.46), channel_id=1, source_target_pairs={{0,2},{2,4},{4,6},{6,8},{8,10},{10,12},{12,14},{1,3},{3,5},{5,7},{... | collective-permute-start | bytes 663560 | tf_op jit(solution)/shard_map/ppermute | solution.py:28
  67.2 4.8 %collective-permute-start.9 = (f32[2,48,576]{2,1,0:T(8,128)S(1)}, f32[2,48,576]{2,1,0:T(8,128)S(1)}, u32[]{:S(2)}, u32[]{:S(2)}) collective-permute-start(f32[2,48,576]{2,1,0:T(8,128)S(1)} %get-tuple-element.46), channel_id=1, source_target_pairs={{2,0},{4,2},{6,4},{8,6},{10,8},{12,10},{14,12},{3,1},{5,3},{7,5},{... | collective-permute-start | bytes 663560 | tf_op jit(solution)/shard_map/ppermute | solution.py:29
  72.0 0.9 fusion.119
  73.0 3.9 %collective-permute-done.8 = f32[2,48,576]{2,1,0:T(8,128)S(1)} collective-permute-done((f32[2,48,576]{2,1,0:T(8,128)S(1)}, f32[2,48,576]{2,1,0:T(8,128)S(1)}, u32[]{:S(2)}, u32[]{:S(2)}) %collective-permute-start.8) | collective-permute-done | bytes 221216 | tf_op jit(solution)/shard_map/ppermute | solution.py:28
  76.8 5.2 %collective-permute-done.9 = f32[2,48,576]{2,1,0:T(8,128)S(1)} collective-permute-done((f32[2,48,576]{2,1,0:T(8,128)S(1)}, f32[2,48,576]{2,1,0:T(8,128)S(1)}, u32[]{:S(2)}, u32[]{:S(2)}) %collective-permute-start.9) | collective-permute-done | bytes 221216 | tf_op jit(solution)/shard_map/ppermute | solution.py:29
  82.0 0.7 pad_maximum_fusion.37
  82.7 2.6 %collective-permute-start.10 = (f32[6,2,576]{2,1,0:T(2,128)}, f32[6,2,576]{2,1,0:T(2,128)}, u32[]{:S(2)}, u32[]{:S(2)}) collective-permute-start(f32[6,2,576]{2,1,0:T(2,128)} %get-tuple-element.52), channel_id=1, source_target_pairs={{0,1},{2,3},{4,5},{6,7},{8,9},{10,11},{12,13},{14,15},{16,17},{18,... | collective-permute-start | bytes 82952 | tf_op jit(solution)/shard_map/ppermute | solution.py:28
  85.3 1.3 collective-permute-start.11
  86.6 2.1 %convolution_multiply_fusion.1 = f32[96,576]{1,0:T(8,128)} fusion(bf16[512,576]{0,1:T(8,128)(2,1)S(1)} %copy-done, f32[96,512]{1,0:T(8,128)} %fusion.119, bf16[96,576]{1,0:T(8,128)(2,1)S(1)} %bitcast.65, bf16[576,512]{1,0:T(8,128)(2,1)S(1)} %copy-done.2), kind=kOutput, calls=%fused_computation.3 | convolution fusion | flops 113399808 | bytes 1708032 | tf_op jit(solution)/shard_map/dot_general | solution.py:112
  88.7 1.1 pad_maximum_fusion.1
  90.4 0.7 copy-done.10
  91.3 1.9 %collective-permute-start.12 = (f32[2,48,576]{2,1,0:T(8,128)S(1)}, f32[2,48,576]{2,1,0:T(8,128)S(1)}, u32[]{:S(2)}, u32[]{:S(2)}) collective-permute-start(f32[2,48,576]{2,1,0:T(8,128)S(1)} %get-tuple-element.44), channel_id=1, source_target_pairs={{0,2},{2,4},{4,6},{6,8},{8,10},{10,12},{12,14},{1,3},{3,5},{5,7},{... | collective-permute-start | bytes 663560 | tf_op jit(solution)/shard_map/ppermute | solution.py:28
  93.2 4.8 %collective-permute-start.13 = (f32[2,48,576]{2,1,0:T(8,128)S(1)}, f32[2,48,576]{2,1,0:T(8,128)S(1)}, u32[]{:S(2)}, u32[]{:S(2)}) collective-permute-start(f32[2,48,576]{2,1,0:T(8,128)S(1)} %get-tuple-element.44), channel_id=1, source_target_pairs={{2,0},{4,2},{6,4},{8,6},{10,8},{12,10},{14,12},{3,1},{5,3},{7,5},{... | collective-permute-start | bytes 663560 | tf_op jit(solution)/shard_map/ppermute | solution.py:29
  98.1 0.9 fusion.120
  99.0 3.3 %collective-permute-done.12 = f32[2,48,576]{2,1,0:T(8,128)S(1)} collective-permute-done((f32[2,48,576]{2,1,0:T(8,128)S(1)}, f32[2,48,576]{2,1,0:T(8,128)S(1)}, u32[]{:S(2)}, u32[]{:S(2)}) %collective-permute-start.12) | collective-permute-done | bytes 221216 | tf_op jit(solution)/shard_map/ppermute | solution.py:28
  102.3 5.8 %collective-permute-done.13 = f32[2,48,576]{2,1,0:T(8,128)S(1)} collective-permute-done((f32[2,48,576]{2,1,0:T(8,128)S(1)}, f32[2,48,576]{2,1,0:T(8,128)S(1)}, u32[]{:S(2)}, u32[]{:S(2)}) %collective-permute-start.13) | collective-permute-done | bytes 221216 | tf_op jit(solution)/shard_map/ppermute | solution.py:29
  108.1 0.7 pad_maximum_fusion.34
  108.8 2.0 %collective-permute-start.14 = (f32[6,2,576]{2,1,0:T(2,128)}, f32[6,2,576]{2,1,0:T(2,128)S(1)}, u32[]{:S(2)}, u32[]{:S(2)}) collective-permute-start(f32[6,2,576]{2,1,0:T(2,128)} %get-tuple-element.50), channel_id=1, source_target_pairs={{0,1},{2,3},{4,5},{6,7},{8,9},{10,11},{12,13},{14,15},{16,17},{18,... | collective-permute-start | bytes 82952 | tf_op jit(solution)/shard_map/ppermute | solution.py:28
  110.9 1.4 collective-permute-start.15
  112.3 1.4 convolution_multiply_fusion
  115.0 0.8 copy-done.4
  116.4 0.6 fusion.121
  117.1 8.5 %all-reduce.2 = (f32[96,40]{0,1:T(8,128)S(1)}, f32[96,40]{0,1:T(8,128)S(1)}) all-reduce(f32[96,40]{0,1:T(8,128)S(1)} %fusion.121, f32[96,40]{0,1:T(8,128)S(1)} %fusion.122), channel_id=2, replica_groups=mesh['grp'=2,'gx'=8,'gy'=2] {'grp'}, use_global_device_ids=true, to_apply=%region_0.2.clone | all-reduce | flops 7680 | bytes 61440
  125.9 4.5 %all_gather.20 = f32[2,48,40]{1,0,2:T(2,128)S(1)} all-gather(f32[2,48,20]{1,0,2:T(2,128)S(1)} %copy.304), channel_id=1, replica_groups=mesh['grp'=2,'gx'=8,'gy'=2] {'grp'}, dimensions={2}, use_global_device_ids=true | all-gather | bytes 23040 | tf_op jit(solution)/shard_map/all_gather | solution.py:160
  130.3 4.5 %all_gather.21 = f32[2,48,40]{1,0,2:T(2,128)S(1)} all-gather(f32[2,48,20]{1,0,2:T(2,128)S(1)} %copy.309), channel_id=1, replica_groups=mesh['grp'=2,'gx'=8,'gy'=2] {'grp'}, dimensions={2}, use_global_device_ids=true | all-gather | bytes 23040 | tf_op jit(solution)/shard_map/all_gather | solution.py:161
  135.2 1.9 %collective-permute-start.20 = (f32[1,48,40]{1,2,0:T(8,128)S(1)}, f32[1,48,40]{1,2,0:T(8,128)S(1)}, u32[]{:S(2)}, u32[]{:S(2)}) collective-permute-start(f32[1,48,40]{1,2,0:T(8,128)S(1)} %get-tuple-element.79), channel_id=1, source_target_pairs={{2,0},{4,2},{6,4},{8,6},{10,8},{12,10},{14,12},{3,1},{5,3},{7,5},{... | collective-permute-start | bytes 23048 | tf_op jit(solution)/shard_map/ppermute | solution.py:29
  137.1 3.9 %collective-permute-start.21 = (f32[1,48,40]{1,2,0:T(8,128)S(1)}, f32[1,48,40]{1,2,0:T(8,128)S(1)}, u32[]{:S(2)}, u32[]{:S(2)}) collective-permute-start(f32[1,48,40]{1,2,0:T(8,128)S(1)} %get-tuple-element.78), channel_id=1, source_target_pairs={{0,2},{2,4},{4,6},{6,8},{8,10},{10,12},{12,14},{1,3},{3,5},{5,7},{... | collective-permute-start | bytes 23048 | tf_op jit(solution)/shard_map/ppermute | solution.py:28
  141.0 2.6 %collective-permute-done.21 = f32[1,48,40]{1,2,0:T(8,128)S(1)} collective-permute-done((f32[1,48,40]{1,2,0:T(8,128)S(1)}, f32[1,48,40]{1,2,0:T(8,128)S(1)}, u32[]{:S(2)}, u32[]{:S(2)}) %collective-permute-start.21) | collective-permute-done | bytes 7712 | tf_op jit(solution)/shard_map/ppermute | solution.py:28
  143.8 1.3 collective-permute-start.22
  145.1 3.0 %collective-permute-start.23 = (f32[4,1,40]{1,2,0:T(8,128)S(1)}, f32[4,1,40]{1,2,0:T(8,128)S(1)}, u32[]{:S(2)}, u32[]{:S(2)}) collective-permute-start(f32[4,1,40]{1,2,0:T(8,128)S(1)} %get-tuple-element.73), channel_id=1, source_target_pairs={{0,1},{2,3},{4,5},{6,7},{8,9},{10,11},{12,13},{14,15},{16,17},{18,... | collective-permute-start | bytes 1928 | tf_op jit(solution)/shard_map/ppermute | solution.py:28
  148.1 0.9 collective-permute-done.23
  149.2 4.5 %all_gather.23 = f32[2,48,40]{1,0,2:T(2,128)S(1)} all-gather(f32[2,48,20]{1,0,2:T(2,128)S(1)} %copy.315), channel_id=1, replica_groups=mesh['grp'=2,'gx'=8,'gy'=2] {'grp'}, dimensions={2}, use_global_device_ids=true | all-gather | bytes 23040 | tf_op jit(solution)/shard_map/all_gather | solution.py:161
  154.4 4.5 %all_gather.22 = f32[2,48,40]{1,0,2:T(2,128)S(1)} all-gather(f32[2,48,20]{1,0,2:T(2,128)S(1)} %copy.312), channel_id=1, replica_groups=mesh['grp'=2,'gx'=8,'gy'=2] {'grp'}, dimensions={2}, use_global_device_ids=true | all-gather | bytes 23040 | tf_op jit(solution)/shard_map/all_gather | solution.py:160
  (143 shorter events, 12.3 us)
Async XLA Ops:
  0.6 32.0 %copy-start = (bf16[512,576]{0,1:T(8,128)(2,1)S(1)}, bf16[512,576]{0,1:T(8,128)(2,1)}, u32[]{:S(2)}) copy-start(bf16[512,576]{0,1:T(8,128)(2,1)} %param.22) | copy-start | bytes 1769476
  0.6 0.7 copy-start.29
  0.7 0.8 copy-start.17
  6.0 0.7 copy-start.26
  7.1 0.8 copy-start.18
  12.4 7.8 %copy-start.28 = (s32[2,48]{1,0:T(2,128)S(1)}, s32[2,48]{1,0:T(2,128)}, u32[]{:S(2)}) copy-start(s32[2,48]{1,0:T(2,128)} %param.14) | copy-start | bytes 1156
  12.4 7.8 %copy-start.13 = (f32[2,48,576]{2,1,0:T(8,128)S(1)}, f32[2,48,576]{2,1,0:T(8,128)}, u32[]{:S(2)}) copy-start(f32[2,48,576]{2,1,0:T(8,128)} %param.13) | copy-start | bytes 663556
  13.0 19.4 %copy-start.1 = (bf16[576,512]{1,0:T(8,128)(2,1)S(1)}, bf16[576,512]{1,0:T(8,128)(2,1)}, u32[]{:S(2)}) copy-start(bf16[576,512]{1,0:T(8,128)(2,1)} %param.20) | copy-start | bytes 1769476
  13.4 37.1 %collective-permute-start.4 = (f32[2,48,32]{1,0,2:T(2,128)S(1)}, f32[2,48,32]{1,0,2:T(2,128)}, u32[]{:S(2)}, u32[]{:S(2)}) collective-permute-start(f32[2,48,32]{1,0,2:T(2,128)S(1)} %constant_dynamic-update-slice_fusion), channel_id=1, source_target_pairs={{0,2},{2,4},{4,6},{6,8},{8,10},{10,12},{12,14},{1,3},{3,5},{5,7},{... | collective-permute-start | bytes 36872 | tf_op jit(solution)/shard_map/ppermute | solution.py:28
  16.8 33.7 %collective-permute-start.5 = (f32[2,48,32]{1,0,2:T(2,128)S(1)}, f32[2,48,32]{1,0,2:T(2,128)}, u32[]{:S(2)}, u32[]{:S(2)}) collective-permute-start(f32[2,48,32]{1,0,2:T(2,128)S(1)} %constant_dynamic-update-slice_fusion), channel_id=1, source_target_pairs={{2,0},{4,2},{6,4},{8,6},{10,8},{12,10},{14,12},{3,1},{5,3},{7,5},{... | collective-permute-start | bytes 36872 | tf_op jit(solution)/shard_map/ppermute | solution.py:29
  20.2 0.5 copy-start.19
  20.2 12.2 %copy-start.27 = (f32[40,32]{0,1:T(8,128)S(1)}, f32[40,32]{0,1:T(8,128)}, u32[]{:S(2)}) copy-start(f32[40,32]{0,1:T(8,128)} %param.19) | copy-start | bytes 15364
  20.7 12.0 %copy-start.2 = (bf16[576,512]{1,0:T(8,128)(2,1)S(1)}, bf16[576,512]{1,0:T(8,128)(2,1)}, u32[]{:S(2)}) copy-start(bf16[576,512]{1,0:T(8,128)(2,1)} %param.21) | copy-start | bytes 1769476
  20.7 33.3 %collective-permute-start = (f32[2,48,576]{2,1,0:T(8,128)S(1)}, f32[2,48,576]{2,1,0:T(8,128)S(1)}, u32[]{:S(2)}, u32[]{:S(2)}) collective-permute-start(f32[2,48,576]{2,1,0:T(8,128)S(1)} %get-tuple-element.49), channel_id=1, source_target_pairs={{0,2},{2,4},{4,6},{6,8},{8,10},{10,12},{12,14},{1,3},{3,5},{5,7},{... | collective-permute-start | bytes 663560 | tf_op jit(solution)/shard_map/ppermute | solution.py:28
  24.6 11.1 %collective-permute-start.16 = (f32[1,48,40]{1,2,0:T(8,128)}, f32[1,48,40]{1,2,0:T(8,128)}, u32[]{:S(2)}, u32[]{:S(2)}) collective-permute-start(f32[1,48,40]{1,2,0:T(8,128)} %get-tuple-element.81), channel_id=1, source_target_pairs={{2,0},{4,2},{6,4},{8,6},{10,8},{12,10},{14,12},{3,1},{5,3},{7,5},{... | collective-permute-start | bytes 23048 | tf_op jit(solution)/shard_map/ppermute | solution.py:29
  28.2 7.4 %collective-permute-start.17 = (f32[1,48,40]{1,2,0:T(8,128)}, f32[1,48,40]{1,2,0:T(8,128)}, u32[]{:S(2)}, u32[]{:S(2)}) collective-permute-start(f32[1,48,40]{1,2,0:T(8,128)} %get-tuple-element.80), channel_id=1, source_target_pairs={{0,2},{2,4},{4,6},{6,8},{8,10},{10,12},{12,14},{1,3},{3,5},{5,7},{... | collective-permute-start | bytes 23048 | tf_op jit(solution)/shard_map/ppermute | solution.py:28
  37.1 8.4 %collective-permute-start.18 = (f32[4,1,40]{1,2,0:T(8,128)}, f32[4,1,40]{1,2,0:T(8,128)}, u32[]{:S(2)}, u32[]{:S(2)}) collective-permute-start(f32[4,1,40]{1,2,0:T(8,128)} %get-tuple-element.76), channel_id=1, source_target_pairs={{1,0},{3,2},{5,4},{7,6},{9,8},{11,10},{13,12},{15,14},{17,16},{19,... | collective-permute-start | bytes 1928 | tf_op jit(solution)/shard_map/ppermute | solution.py:29
  38.4 11.1 %collective-permute-start.19 = (f32[4,1,40]{1,2,0:T(8,128)}, f32[4,1,40]{1,2,0:T(8,128)}, u32[]{:S(2)}, u32[]{:S(2)}) collective-permute-start(f32[4,1,40]{1,2,0:T(8,128)} %get-tuple-element.77), channel_id=1, source_target_pairs={{0,1},{2,3},{4,5},{6,7},{8,9},{10,11},{12,13},{14,15},{16,17},{18,... | collective-permute-start | bytes 1928 | tf_op jit(solution)/shard_map/ppermute | solution.py:28
  43.6 0.7 copy-start.30
  45.5 8.5 %collective-permute-start.1 = (f32[2,48,576]{2,1,0:T(8,128)S(1)}, f32[2,48,576]{2,1,0:T(8,128)S(1)}, u32[]{:S(2)}, u32[]{:S(2)}) collective-permute-start(f32[2,48,576]{2,1,0:T(8,128)S(1)} %get-tuple-element.49), channel_id=1, source_target_pairs={{2,0},{4,2},{6,4},{8,6},{10,8},{12,10},{14,12},{3,1},{5,3},{7,5},{... | collective-permute-start | bytes 663560 | tf_op jit(solution)/shard_map/ppermute | solution.py:29
  51.4 8.3 %collective-permute-start.6 = (f32[6,2,32]{1,0,2:T(8,128)S(1)}, f32[6,2,32]{1,0,2:T(8,128)S(1)}, u32[]{:S(2)}, u32[]{:S(2)}) collective-permute-start(f32[6,2,32]{1,0,2:T(8,128)S(1)} %get-tuple-element.68), channel_id=1, source_target_pairs={{0,1},{2,3},{4,5},{6,7},{8,9},{10,11},{12,13},{14,15},{16,17},{18,... | collective-permute-start | bytes 4616 | tf_op jit(solution)/shard_map/ppermute | solution.py:28
  52.7 7.0 %collective-permute-start.7 = (f32[6,2,32]{1,0,2:T(8,128)S(1)}, f32[6,2,32]{1,0,2:T(8,128)S(1)}, u32[]{:S(2)}, u32[]{:S(2)}) collective-permute-start(f32[6,2,32]{1,0,2:T(8,128)S(1)} %get-tuple-element.69), channel_id=1, source_target_pairs={{1,0},{3,2},{5,4},{7,6},{9,8},{11,10},{13,12},{15,14},{17,16},{19,... | collective-permute-start | bytes 4616 | tf_op jit(solution)/shard_map/ppermute | solution.py:29
  54.1 0.8 copy-start.5
  54.1 0.8 copy-start.6
  54.9 6.1 %collective-permute-start.2 = (f32[6,2,576]{2,1,0:T(2,128)}, f32[6,2,576]{2,1,0:T(2,128)}, u32[]{:S(2)}, u32[]{:S(2)}) collective-permute-start(f32[6,2,576]{2,1,0:T(2,128)} %get-tuple-element.54), channel_id=1, source_target_pairs={{0,1},{2,3},{4,5},{6,7},{8,9},{10,11},{12,13},{14,15},{16,17},{18,... | collective-permute-start | bytes 82952 | tf_op jit(solution)/shard_map/ppermute | solution.py:28
  58.5 3.4 %collective-permute-start.3 = (f32[6,2,576]{2,1,0:T(2,128)}, f32[6,2,576]{2,1,0:T(2,128)}, u32[]{:S(2)}, u32[]{:S(2)}) collective-permute-start(f32[6,2,576]{2,1,0:T(2,128)} %get-tuple-element.55), channel_id=1, source_target_pairs={{1,0},{3,2},{5,4},{7,6},{9,8},{11,10},{13,12},{15,14},{17,16},{19,... | collective-permute-start | bytes 82952 | tf_op jit(solution)/shard_map/ppermute | solution.py:29
  61.9 1.2 copy-start.22
  63.1 0.7 copy-start.21
  64.0 0.9 copy-start.11
  64.0 1.1 copy-start.12
  64.3 0.8 copy-start.25
  64.3 0.8 copy-start.24
  64.3 0.8 copy-start.23
  64.3 0.8 copy-start.20
  65.3 11.5 %collective-permute-start.8 = (f32[2,48,576]{2,1,0:T(8,128)S(1)}, f32[2,48,576]{2,1,0:T(8,128)S(1)}, u32[]{:S(2)}, u32[]{:S(2)}) collective-permute-start(f32[2,48,576]{2,1,0:T(8,128)S(1)} %get-tuple-element.46), channel_id=1, source_target_pairs={{0,2},{2,4},{4,6},{6,8},{8,10},{10,12},{12,14},{1,3},{3,5},{5,7},{... | collective-permute-start | bytes 663560 | tf_op jit(solution)/shard_map/ppermute | solution.py:28
  67.2 14.8 %collective-permute-start.9 = (f32[2,48,576]{2,1,0:T(8,128)S(1)}, f32[2,48,576]{2,1,0:T(8,128)S(1)}, u32[]{:S(2)}, u32[]{:S(2)}) collective-permute-start(f32[2,48,576]{2,1,0:T(8,128)S(1)} %get-tuple-element.46), channel_id=1, source_target_pairs={{2,0},{4,2},{6,4},{8,6},{10,8},{12,10},{14,12},{3,1},{5,3},{7,5},{... | collective-permute-start | bytes 663560 | tf_op jit(solution)/shard_map/ppermute | solution.py:29
  82.0 0.7 copy-start.9
  82.7 6.0 %collective-permute-start.10 = (f32[6,2,576]{2,1,0:T(2,128)}, f32[6,2,576]{2,1,0:T(2,128)}, u32[]{:S(2)}, u32[]{:S(2)}) collective-permute-start(f32[6,2,576]{2,1,0:T(2,128)} %get-tuple-element.52), channel_id=1, source_target_pairs={{0,1},{2,3},{4,5},{6,7},{8,9},{10,11},{12,13},{14,15},{16,17},{18,... | collective-permute-start | bytes 82952 | tf_op jit(solution)/shard_map/ppermute | solution.py:28
  85.3 3.4 %collective-permute-start.11 = (f32[6,2,576]{2,1,0:T(2,128)}, f32[6,2,576]{2,1,0:T(2,128)}, u32[]{:S(2)}, u32[]{:S(2)}) collective-permute-start(f32[6,2,576]{2,1,0:T(2,128)} %get-tuple-element.53), channel_id=1, source_target_pairs={{1,0},{3,2},{5,4},{7,6},{9,8},{11,10},{13,12},{15,14},{17,16},{19,... | collective-permute-start | bytes 82952 | tf_op jit(solution)/shard_map/ppermute | solution.py:29
  90.2 0.9 copy-start.10
  91.3 11.0 %collective-permute-start.12 = (f32[2,48,576]{2,1,0:T(8,128)S(1)}, f32[2,48,576]{2,1,0:T(8,128)S(1)}, u32[]{:S(2)}, u32[]{:S(2)}) collective-permute-start(f32[2,48,576]{2,1,0:T(8,128)S(1)} %get-tuple-element.44), channel_id=1, source_target_pairs={{0,2},{2,4},{4,6},{6,8},{8,10},{10,12},{12,14},{1,3},{3,5},{5,7},{... | collective-permute-start | bytes 663560 | tf_op jit(solution)/shard_map/ppermute | solution.py:28
  93.2 14.9 %collective-permute-start.13 = (f32[2,48,576]{2,1,0:T(8,128)S(1)}, f32[2,48,576]{2,1,0:T(8,128)S(1)}, u32[]{:S(2)}, u32[]{:S(2)}) collective-permute-start(f32[2,48,576]{2,1,0:T(8,128)S(1)} %get-tuple-element.44), channel_id=1, source_target_pairs={{2,0},{4,2},{6,4},{8,6},{10,8},{12,10},{14,12},{3,1},{5,3},{7,5},{... | collective-permute-start | bytes 663560 | tf_op jit(solution)/shard_map/ppermute | solution.py:29
  108.1 0.7 copy-start.7
  108.8 4.9 %collective-permute-start.14 = (f32[6,2,576]{2,1,0:T(2,128)}, f32[6,2,576]{2,1,0:T(2,128)S(1)}, u32[]{:S(2)}, u32[]{:S(2)}) collective-permute-start(f32[6,2,576]{2,1,0:T(2,128)} %get-tuple-element.50), channel_id=1, source_target_pairs={{0,1},{2,3},{4,5},{6,7},{8,9},{10,11},{12,13},{14,15},{16,17},{18,... | collective-permute-start | bytes 82952 | tf_op jit(solution)/shard_map/ppermute | solution.py:28
  110.9 3.2 %copy-start.8 = (f32[2,48,576]{2,1,0:T(8,128)S(1)}, f32[2,48,576]{2,1,0:T(8,128)}, u32[]{:S(2)}) copy-start(f32[2,48,576]{2,1,0:T(8,128)} %copy-done.7) | copy-start | bytes 663556
  110.9 3.2 %collective-permute-start.15 = (f32[6,2,576]{2,1,0:T(2,128)S(1)}, f32[6,2,576]{2,1,0:T(2,128)S(1)}, u32[]{:S(2)}, u32[]{:S(2)}) collective-permute-start(f32[6,2,576]{2,1,0:T(2,128)S(1)} %get-tuple-element.51), channel_id=1, source_target_pairs={{1,0},{3,2},{5,4},{7,6},{9,8},{11,10},{13,12},{15,14},{17,16},{19,... | collective-permute-start | bytes 82952 | tf_op jit(solution)/shard_map/ppermute | solution.py:29
  114.8 1.0 copy-start.4
  115.0 1.4 copy-start.3
  125.7 23.4 %copy-start.15 = (f32[2,48,20]{1,0,2:T(2,128)}, f32[2,48,20]{1,0,2:T(2,128)S(1)}, u32[]{:S(2)}) copy-start(f32[2,48,20]{1,0,2:T(2,128)S(1)} %reshape.208) | copy-start | bytes 23044
  125.8 23.3 %copy-start.16 = (f32[2,48,20]{1,0,2:T(2,128)}, f32[2,48,20]{1,0,2:T(2,128)S(1)}, u32[]{:S(2)}) copy-start(f32[2,48,20]{1,0,2:T(2,128)S(1)} %reshape.209) | copy-start | bytes 23044
  130.3 4.5 %copy-start.14 = (f32[40,20]{0,1:T(8,128)S(1)}, f32[40,20]{0,1:T(8,128)}, u32[]{:S(2)}) copy-start(f32[40,20]{0,1:T(8,128)} %param.23) | copy-start | bytes 9604
  135.2 5.9 %collective-permute-start.20 = (f32[1,48,40]{1,2,0:T(8,128)S(1)}, f32[1,48,40]{1,2,0:T(8,128)S(1)}, u32[]{:S(2)}, u32[]{:S(2)}) collective-permute-start(f32[1,48,40]{1,2,0:T(8,128)S(1)} %get-tuple-element.79), channel_id=1, source_target_pairs={{2,0},{4,2},{6,4},{8,6},{10,8},{12,10},{14,12},{3,1},{5,3},{7,5},{... | collective-permute-start | bytes 23048 | tf_op jit(solution)/shard_map/ppermute | solution.py:29
  137.1 6.6 %collective-permute-start.21 = (f32[1,48,40]{1,2,0:T(8,128)S(1)}, f32[1,48,40]{1,2,0:T(8,128)S(1)}, u32[]{:S(2)}, u32[]{:S(2)}) collective-permute-start(f32[1,48,40]{1,2,0:T(8,128)S(1)} %get-tuple-element.78), channel_id=1, source_target_pairs={{0,2},{2,4},{4,6},{6,8},{8,10},{10,12},{12,14},{1,3},{3,5},{5,7},{... | collective-permute-start | bytes 23048 | tf_op jit(solution)/shard_map/ppermute | solution.py:28
  143.8 4.3 %collective-permute-start.22 = (f32[4,1,40]{1,2,0:T(8,128)S(1)}, f32[4,1,40]{1,2,0:T(8,128)S(1)}, u32[]{:S(2)}, u32[]{:S(2)}) collective-permute-start(f32[4,1,40]{1,2,0:T(8,128)S(1)} %get-tuple-element.72), channel_id=1, source_target_pairs={{1,0},{3,2},{5,4},{7,6},{9,8},{11,10},{13,12},{15,14},{17,16},{19,... | collective-permute-start | bytes 1928 | tf_op jit(solution)/shard_map/ppermute | solution.py:29
  145.1 3.9 %collective-permute-start.23 = (f32[4,1,40]{1,2,0:T(8,128)S(1)}, f32[4,1,40]{1,2,0:T(8,128)S(1)}, u32[]{:S(2)}, u32[]{:S(2)}) collective-permute-start(f32[4,1,40]{1,2,0:T(8,128)S(1)} %get-tuple-element.73), channel_id=1, source_target_pairs={{0,1},{2,3},{4,5},{6,7},{8,9},{10,11},{12,13},{14,15},{16,17},{18,... | collective-permute-start | bytes 1928 | tf_op jit(solution)/shard_map/ppermute | solution.py:28
where the time goes:
time: 161 us; the launch traced here: 160 us
  starting transfers between devices  64.3 us (40%)
  blocking collectives  35.2 us (22%)
  waiting for transfers between devices  23.1 us (14%)
  other arithmetic  13.4 us (8%)
  local copies, waits for them, and re-layouts  12.4 us (8%)
  matrix products  9.09 us (6%)
  between operations  2.19 us (1%)
    ppermute x12, starting transfers between devices, extended(): before = lax.ppermute(last, axis, up)  34 us
    ppermute x12, starting transfers between devices, extended(): after = lax.ppermute(leading, axis, down)  30.3 us
    ppermute x12, waiting for transfers between devices, extended(): after = lax.ppermute(leading, axis, down)  12.4 us
    ppermute x12, waiting for transfers between devices, extended(): before = lax.ppermute(last, axis, up)  10.7 us
    all_gather x2, blocking collectives, body(): lax.all_gather(first_v, 'grp', axis=2, tiled=True)  8.9 us
    all_gather x2, blocking collectives, body(): lax.all_gather(first_u, 'grp', axis=2, tiled=True)  8.9 us
    unnamed x1, blocking collectives  8.49 us
    unnamed x70, local copies, waits for them, and re-layouts  7.46 us
  transfers between devices with their start and end apart: 24, of which 8 were waited for; matrix products, arithmetic and copies ran while one was open for 11% of the time, Pallas kernels for 0%

commit v1 on v0

v1 whole, which is shorter than its diff:
```python
import functools

import jax
import jax.numpy as jnp
import numpy as np
from jax import lax
from jax.experimental import pallas as pl
from jax.experimental.pallas import tpu as pltpu
from jax.sharding import PartitionSpec as P

NF = 32
ND = 36
NLEV = 40
WAVE_SECTIONS = 3
NFL = 16
LANES = 128
MESH = pl.DeviceIdType.MESH

highest = lax.Precision.HIGHEST
inter_step = 0.1
ocean_step = 0.4
coriolis = 0.5
viscosity = 0.1


def exact_dot(a, b):
    return jnp.dot(a, b, precision=highest, preferred_element_type=jnp.float32)


def sweep(centre, back_one, back_two, next_one, next_two, velocity):
    up = velocity >= 0.0
    one = jnp.where(up, back_one, next_one)
    two = jnp.where(up, back_two, next_two)
    size = jnp.abs(velocity)
    half = 0.5 * size
    return centre - half * (3.0 * centre - 4.0 * one + two) + half * size * (centre - 2.0 * one + two)


def iota(shape, dim):
    return lax.broadcasted_iota(jnp.int32, shape, dim)


class Move:
    def __init__(self, src, dst, send, recv, device, sends, receives):
        self.copy = pltpu.make_async_remote_copy(
            src_ref=src, dst_ref=dst, send_sem=send, recv_sem=recv, device_id=device, device_id_type=MESH
        )
        self.sends, self.receives = sends, receives

    def when(self, cond, act):
        if cond is True:
            act()
        else:
            pl.when(cond)(act)

    def start(self):
        self.when(self.sends, self.copy.start)

    def wait_send(self):
        self.when(self.sends, self.copy.wait_send)

    def wait_recv(self):
        self.when(self.receives, self.copy.wait_recv)


def kernel(
    sizes,
    spectrum,
    pack,
    angles,
    cw,
    dw,
    left,
    right,
    out_map,
    spec_out,
    u_out,
    v_out,
    du_out,
    dv_out,
    masked,
    packs,
    own_flow,
    flow,
    flow_edge,
    flow_halo,
    field,
    edge,
    halo_x,
    halo_y,
    speed_x,
    speed_y,
    turn,
    speed_l,
    speed_r,
    wide,
    source,
    mix,
    ocean,
    ocean_next,
    row_halo,
    col_edge,
    col_halo,
    drift_q,
    drift_n,
    init_send,
    init_recv,
    wave_send,
    wave_recv,
    sea_send,
    sea_recv,
):
    nx, ny = sizes
    tile_x, tile_y, bins = spectrum.shape
    half = tile_y // 2
    own = u_out.shape[2]
    rows = 2 * tile_x
    g, gx, gy = lax.axis_index("grp"), lax.axis_index("gx"), lax.axis_index("gy")
    z, y = gx // 2, gx % 2
    q = 2 * gy + y
    nz, nq = nx // 2, 2 * ny

    def at(dg=0, x=gx, c=gy):
        return {"grp": (g + dg) % 2, "gx": x, "gy": c}

    pair = 2 * z + 1 - y

    def q_at(dz, dq):
        qq = q + dq
        return at(0, 2 * (z + dz) + qq % 2, qq // 2)

    def inside(value, step, limit):
        return value + step >= 0 if step < 0 else value + step < limit

    def both(dz, dq):
        cond = inside(q, dq, nq)
        return cond if dz == 0 else cond & inside(z, dz, nz)

    friends = [(True, at(1)), (True, at(0, pair)), (True, at(1, pair))]
    friends += [(inside(z, d, nz), at(0, gx + 2 * d)) for d in (-1, 1)]
    friends += [(both(dz, dq), q_at(dz, dq)) for dq in (-1, 1) for dz in (-1, 0, 1)]
    friends += [(inside(gx, d, nx), at(0, gx + d)) for d in (-1, 1)]
    friends += [(inside(gy, d, ny), at(0, gx, gy + d)) for d in (-1, 1)]
    barrier = pltpu.get_barrier_semaphore()
    total = 0
    for cond, device in friends:

        def hello(device=device):
            pl.semaphore_signal(barrier, inc=1, device_id=device, device_id_type=MESH)

        if cond is True:
            hello()
            total = total + 1
        else:
            pl.when(cond)(hello)
            total = total + jnp.where(cond, 1, 0)

    columns = tile_x * tile_y
    wet_n = pack[0:columns, 2 * own : 2 * own + 1]
    masked[...] = (spectrum[...].reshape(columns, bins) * wet_n).reshape(tile_x, tile_y, bins)

    @pl.when(z == 0)
    def _():
        halo_x[:, 0] = jnp.zeros_like(halo_x[:, 0])

    @pl.when(z == nz - 1)
    def _():
        halo_x[:, 1] = jnp.zeros_like(halo_x[:, 1])

    for side, dq in ((0, -1), (1, 1)):

        @pl.when(jnp.logical_not(inside(q, dq, nq)))
        def _():
            halo_y[:, side] = jnp.zeros_like(halo_y[:, side])
            flow_halo[side] = jnp.zeros_like(flow_halo[side])

        for slot, dz in ((0, -1), (2, 1)):

            @pl.when(inside(q, dq, nq) & jnp.logical_not(inside(z, dz, nz)))
            def _():
                halo_y[:, side, slot] = jnp.zeros_like(halo_y[:, side, slot])

    for side, d in ((0, -1), (1, 1)):

        @pl.when(jnp.logical_not(inside(gx, d, nx)))
        def _():
            row_halo[:, side] = jnp.zeros_like(row_halo[:, side])

        @pl.when(jnp.logical_not(inside(gy, d, ny)))
        def _():
            col_halo[:, side] = jnp.zeros_like(col_halo[:, side])

    pl.semaphore_wait(barrier, total)

    to_grp = Move(pack, packs, init_send.at[0], init_recv.at[0], at(1), True, True)
    to_grp.start()
    away = pl.ds(pl.multiple_of(half * (1 - y), 8), half)
    mine = pl.ds(pl.multiple_of(half * y, 8), half)
    my_rows = pl.ds(tile_x * y, tile_x)
    to_pair = Move(
        masked.at[:, away, :], field.at[my_rows], init_send.at[1], init_recv.at[1], at(0, pair), True, True
    )
    to_pair.start()
    field[my_rows] = masked[:, mine, :]

    place_i, place_j = iota((LANES, LANES), 0), iota((LANES, LANES), 1)

    def placing(group):
        shift = own * group + jnp.where(place_i < own, 0, own)
        keep = (place_i < 2 * own) & (place_j == place_i + shift)
        return jnp.where(keep, 1.0, 0.0)

    to_grp.wait_recv()
    everything = exact_dot(pack[...], placing(g)) + exact_dot(packs[...], placing(1 - g))
    ocean[...] = everything[:columns].reshape(ocean.shape)
    mix[...] = jnp.zeros_like(mix)
    mix[0:NLEV] = everything[columns:]
    mix[NLEV : 2 * NLEV] = pltpu.roll(everything[columns:], NLEV, 1)
    chosen = jnp.where(iota((columns, columns), 1).astype(jnp.float32) == pack[0:columns, 2 * own + 1 : 2 * own + 2], 1.0, 0.0)
    felt = exact_dot(chosen, exact_dot(everything[:columns], cw[...]))
    felt = felt + jnp.where(iota((columns, LANES), 1) == 2 * NF, wet_n, 0.0)
    own_flow[...] = felt.reshape(own_flow.shape)
    flow_pair = Move(
        own_flow.at[:, away, :], flow.at[my_rows], init_send.at[2], init_recv.at[2], at(0, pair), True, True
    )
    flow_pair.start()
    flow[my_rows] = own_flow[:, mine, :]

    def sea_moves(k, array):
        moves = []
        for side, d in ((0, -1), (1, 1)):
            moves.append(
                Move(
                    array.at[0 if d < 0 else tile_x - 1],
                    row_halo.at[k, 1 - side],
                    sea_send.at[k, side],
                    sea_recv.at[k, side],
                    at(0, gx + d),
                    inside(gx, d, nx),
                    inside(gx, -d, nx),
                )
            )
            moves.append(
                Move(
                    col_edge.at[k, side],
                    col_halo.at[k, 1 - side],
                    sea_send.at[k, 2 + side],
                    sea_recv.at[k, 2 + side],
                    at(0, gx, gy + d),
                    inside(gy, d, ny),
                    inside(gy, -d, ny),
                )
            )
        return moves

    def set_col_edges(k, array):
        for side, column in ((0, 0), (1, tile_y - 1)):
            for r in range(tile_x):
                col_edge[k, side, r : r + 1, :] = array[r, column : column + 1, :]

    lane = iota((1, bins), 1)
    frequency = (g * NFL + (lane & (NFL - 1))).astype(jnp.float32)
    group_speed = 0.2 + 0.4 * (NF - 1 - frequency) / (NF - 1)
    turning = 0.5 * (frequency + 1.0) / NF
    cosine, sine = angles[0:1, :], angles[1:2, :]
    spread_i = iota((LANES, bins), 0)
    spread_f = g * NFL + (iota((LANES, bins), 1) & (NFL - 1))
    spread_x = jnp.where(spread_i == spread_f, 1.0, 0.0)
    spread_y = jnp.where(spread_i == spread_f + NF, 1.0, 0.0)

    def wave_moves(s):
        moves = []
        for side, dz in ((0, -1), (1, 1)):
            moves.append(
                Move(
                    field.at[pl.ds(0 if dz < 0 else rows - 2, 2)],
                    halo_x.at[s, 1 - side],
                    wave_send.at[s, side],
                    wave_recv.at[s, side],
                    at(0, gx + 2 * dz),
                    inside(z, dz, nz),
                    inside(z, -dz, nz),
                )
            )
        k = 2
        for side, dq in ((0, -1), (1, 1)):
            for dz in (-1, 0, 1):
                moves.append(
                    Move(
                        edge.at[s, side],
                        halo_y.at[s, 1 - side, 1 - dz],
                        wave_send.at[s, k],
                        wave_recv.at[s, k],
                        q_at(dz, dq),
                        both(dz, dq),
                        both(-dz, -dq),
                    )
                )
                k += 1
        return moves

    def set_edges(s):
        for side, first in ((0, 0), (1, half - 2)):
            for r in range(rows):
                edge[s, side, 2 * r : 2 * r + 2, :] = field[r, first : first + 2, :]

    def interaction():
        now = field[...].reshape(rows * half, bins).astype(jnp.bfloat16)
        product = jnp.dot(now, left[...], preferred_element_type=jnp.float32) * jnp.dot(
            now, right[...], preferred_element_type=jnp.float32
        )
        result = jnp.dot(product.astype(jnp.bfloat16), out_map[...], preferred_element_type=jnp.float32)
        source[...] = (inter_step * result).reshape(source.shape)

    def finish(s, moves):
        for m in moves:
            m.wait_recv()
        for side, speed, start in ((0, speed_l, 6), (1, speed_r, half + 8)):
            before, here, after = (halo_y[s, side, i] for i in range(3))
            low = iota((8, bins), 0)

            def joined(a, b, n):
                return jnp.where(low < n, pltpu.roll(a, n, 0), pltpu.roll(b, n, 0))

            packed = sweep(
                here,
                joined(before, here, 2),
                joined(before, here, 4),
                joined(here, after, 6),
                joined(here, after, 4),
                speed[...],
            )
            for r in range(rows):
                wide[r, start : start + 2, :] = packed[2 * r : 2 * r + 2]

        def line(r):
            if r < 0:
                return halo_x[s, 0, r + 2]
            if r >= rows:
                return halo_x[s, 1, r - rows]
            return field[r]

        for r in range(rows):
            wide[r, 8 : 8 + half, :] = sweep(
                line(r), line(r - 1), line(r - 2), line(r + 1), line(r + 2), speed_x[r]
            )
        for m in moves:
            m.wait_send()
        for r in range(rows):
            b = sweep(
                wide[r, 8 : 8 + half, :],
                wide[r, 7 : 7 + half, :],
                wide[r, 6 : 6 + half, :],
                wide[r, 9 : 9 + half, :],
                wide[r, 10 : 10 + half, :],
                speed_y[r],
            )
            t = turn[r]
            behind = jnp.concatenate([b[:, bins - NFL :], b[:, : bins - NFL]], axis=1)
            ahead = jnp.concatenate([b[:, NFL:], b[:, :NFL]], axis=1)
            c = b - jnp.abs(t) * (b - jnp.where(t >= 0.0, behind, ahead))
            field[r] = flow[r, :, 2 * NF : 2 * NF + 1] * (c + source[r])

    def flow_moves():
        return [
            Move(
                flow_edge.at[side],
                flow_halo.at[1 - side],
                init_send.at[3 + side],
                init_recv.at[3 + side],
                q_at(0, dq),
                inside(q, dq, nq),
                inside(q, -dq, nq),
            )
            for side, dq in ((0, -1), (1, 1))
        ]

    to_pair.wait_recv()
    set_edges(0)
    first_moves = wave_moves(0)
    for m in first_moves:
        m.start()
    set_col_edges(0, ocean)
    flow_pair.wait_recv()
    for side, first in ((0, 0), (1, half - 2)):
        for r in range(rows):
            flow_edge[side, 2 * r : 2 * r + 2, :] = flow[r, first : first + 2, :]
    edges_flow = flow_moves()
    for m in edges_flow:
        m.start()
    sea_first = sea_moves(0, ocean)
    for m in sea_first:
        m.start()
    fq = flow[...].reshape(rows * half, LANES)
    fx = exact_dot(fq, spread_x)
    fy = exact_dot(fq, spread_y)
    speed_x[...] = (group_speed * cosine + fx).reshape(speed_x.shape)
    speed_y[...] = (group_speed * sine + fy).reshape(speed_x.shape)
    turn[...] = (turning * (sine * fx - cosine * fy)).reshape(speed_x.shape)
    interaction()
    for m in edges_flow:
        m.wait_recv()
    speed_l[...] = group_speed * cosine + exact_dot(flow_halo[0], spread_x)
    speed_r[...] = group_speed * cosine + exact_dot(flow_halo[1], spread_x)
    finish(0, first_moves)

    def section(s, carry):
        set_edges(s)
        moves = wave_moves(s)
        for m in moves:
            m.start()
        interaction()
        finish(s, moves)
        return carry

    lax.fori_loop(1, WAVE_SECTIONS, section, 0)

    their_rows = pl.ds(tile_x * (1 - y), tile_x)
    back = Move(
        field.at[their_rows], spec_out.at[:, mine, :], init_send.at[5], init_recv.at[5], at(0, pair), True, True
    )
    depth = exact_dot(dw[...], spread_x)
    unused = jnp.zeros((LANES - 2 * NLEV, bins), jnp.float32)
    profile = jnp.concatenate([depth * cosine, depth * sine, unused], axis=0)
    drift = lax.dot_general(
        field[...].reshape(rows * half, bins),
        profile,
        (((1,), (1,)), ((), ())),
        precision=highest,
        preferred_element_type=jnp.float32,
    )
    drift_q[...] = drift.reshape(drift_q.shape)
    drift_moves = [
        Move(
            drift_q.at[pl.ds(tile_x * yy, tile_x)],
            drift_n.at[g, :, mine, :],
            init_send.at[6 + k],
            init_recv.at[6 + k],
            device,
            True,
            True,
        )
        for k, (yy, device) in enumerate(((y, at(1)), (1 - y, at(1, pair)), (1 - y, at(0, pair))))
    ]
    for m in drift_moves:
        m.start()
    back.start()
    spec_out[:, mine, :] = field[my_rows]
    drift_n[g, :, mine, :] = drift_q[my_rows]

    lane_n = iota((columns, LANES), 1)
    column_n = iota((tile_y, LANES), 0)

    def neighbours(k, array):
        result = []
        for r in range(tile_x):
            a = array[r]
            below = array[r - 1] if r > 0 else row_halo[k, 0]
            above = array[r + 1] if r < tile_x - 1 else row_halo[k, 1]
            lower = jnp.where(column_n == 0, col_halo[k, 0, r : r + 1, :], pltpu.roll(a, 1, 0))
            upper = jnp.where(column_n == tile_y - 1, col_halo[k, 1, r : r + 1, :], pltpu.roll(a, tile_y - 1, 0))
            result.append(above + below + upper + lower - 4.0 * a)
        return jnp.concatenate(result, axis=0)

    def swapped(a):
        from_v = pltpu.roll(a, LANES - NLEV, 1)
        from_u = pltpu.roll(a, NLEV, 1)
        return jnp.where(lane_n < NLEV, from_v, jnp.where(lane_n < 2 * NLEV, -from_u, 0.0))

    def ocean_section(array, laplace, drift_all):
        flat = array[...].reshape(columns, LANES)
        first = flat + ocean_step * (coriolis * swapped(flat + drift_all) + viscosity * laplace)
        return wet_n * (first + exact_dot(first, mix[...]))

    for m in sea_first:
        m.wait_recv()
    laplace_first = neighbours(0, ocean)
    for k, device in enumerate((at(1), at(1, pair), at(0, pair))):
        landing = drift_n.at[1 - g if k < 2 else g, :, mine if k == 0 else away, :]
        Move(drift_q.at[my_rows], landing, init_send.at[6 + k], init_recv.at[6 + k], device, True, True).wait_recv()
    drift_all = (drift_n[0] + drift_n[1]).reshape(columns, LANES)
    ocean_next[...] = ocean_section(ocean, laplace_first, drift_all).reshape(ocean.shape)
    set_col_edges(1, ocean_next)
    sea_second = sea_moves(1, ocean_next)
    for m in sea_second:
        m.start()

    def picking(offset):
        i, j = iota((LANES, own), 0), iota((LANES, own), 1)
        return jnp.where(i == j + own * g + offset, 1.0, 0.0)

    shape = u_out.shape
    pick_u, pick_v = picking(0), picking(NLEV)
    du_out[...] = exact_dot(drift_all, pick_u).reshape(shape)
    dv_out[...] = exact_dot(drift_all, pick_v).reshape(shape)
    for m in sea_second:
        m.wait_recv()
    final = ocean_section(ocean_next, neighbours(1, ocean_next), drift_all)
    u_out[...] = exact_dot(final, pick_u).reshape(shape)
    v_out[...] = exact_dot(final, pick_v).reshape(shape)
    back.wait_recv()
    for m in [to_grp, to_pair, flow_pair, back] + edges_flow + drift_moves + sea_first + sea_second:
        m.wait_send()


def solution(mesh):
    sizes = (mesh.shape["gx"], mesh.shape["gy"])
    theta = 2.0 * np.pi * np.arange(ND) / ND
    table = np.zeros((8, ND * NFL), np.float32)
    table[0] = np.repeat(np.cos(theta), NFL)
    table[1] = np.repeat(np.sin(theta), NFL)

    def body(spectrum, wet_mask, ocean_source, ocean_u, ocean_v, current_weights, drift_weights, inter_left, inter_right, inter_out, mixing):
        tile_x, tile_y, bins = spectrum.shape
        half, rows = tile_y // 2, 2 * tile_x
        own = ocean_u.shape[2]
        columns = tile_x * tile_y
        f32 = jnp.float32
        pack = jnp.concatenate(
            [
                ocean_u.reshape(columns, own),
                ocean_v.reshape(columns, own),
                wet_mask.astype(f32).reshape(columns, 1),
                ocean_source.astype(f32).reshape(columns, 1),
                jnp.zeros((columns, LANES - 2 * own - 2), f32),
            ],
            axis=1,
        )
        pack = jnp.concatenate([pack, jnp.pad(mixing, ((0, 0), (0, LANES - own)))], axis=0)
        low = NLEV
        cw = jnp.pad(current_weights, ((0, LANES - low), (0, LANES - NF))) + jnp.pad(
            current_weights, ((low, LANES - 2 * low), (NF, LANES - 2 * NF))
        )
        dw = jnp.pad(drift_weights, ((0, 64 - low), (0, LANES - NF)))[:low]
        vmem = pl.BlockSpec(memory_space=pltpu.VMEM)
        sea = (tile_x, tile_y, LANES)
        sections = WAVE_SECTIONS
        wave = (rows, half, bins)

        def V(*shape):
            return pltpu.VMEM(shape, f32)

        def D(*shape):
            return pltpu.SemaphoreType.DMA(shape)

        small = jax.ShapeDtypeStruct(ocean_u.shape, f32)
        return pl.pallas_call(
            functools.partial(kernel, sizes),
            out_shape=(jax.ShapeDtypeStruct(spectrum.shape, f32), small, small, small, small),
            in_specs=[vmem] * 8,
            out_specs=(vmem,) * 5,
            scratch_shapes=[
                V(tile_x, tile_y, bins),
                V(columns + NLEV, LANES),
                V(*sea),
                V(rows, half, LANES),
                V(2, 8, LANES),
                V(2, 8, LANES),
                V(*wave),
                V(sections, 2, 8, bins),
                V(sections, 2, 2, half, bins),
                V(sections, 2, 3, 8, bins),
                V(*wave),
                V(*wave),
                V(*wave),
                V(8, bins),
                V(8, bins),
                V(rows, half + 16, bins),
                V(*wave),
                V(LANES, LANES),
                V(*sea),
                V(*sea),
                V(2, 2, tile_y, LANES),
                V(2, 2, 8, LANES),
                V(2, 2, 8, LANES),
                V(rows, half, LANES),
                V(2, *sea),
                D(9),
                D(9),
                D(sections, 8),
                D(sections, 8),
                D(2, 4),
                D(2, 4),
            ],
            compiler_params=pltpu.CompilerParams(collective_id=0, has_side_effects=True, vmem_limit_bytes=40 * 2**20),
        )(spectrum, pack, jnp.asarray(table), cw, dw, inter_left, inter_right, inter_out)

    tile = P("gx", "gy", "grp")
    in_specs = (
        tile,
        P("gx", "gy"),
        P("gx", "gy"),
        tile,
        tile,
        P(),
        P(),
        P("grp", None),
        P("grp", None),
        P(None, "grp"),
        P(None, "grp"),
    )
    return jax.shard_map(body, mesh=mesh, in_specs=in_specs, out_specs=(tile,) * 5, check_vma=False)
```

time: 161 us -> 48.7 us (0.30)
  the two profiles are of different devices: /device:TPU:24 before, /device:TPU:0 now
where the time goes in v1:
time: 48.7 us; the launch traced here: 48.3 us
  Pallas kernels  37 us (76%)
  local copies, waits for them, and re-layouts  9.07 us (19%)
  other arithmetic  1.51 us (3%)
  between operations  0.73 us (1%)
    pallas_call x1, Pallas kernels, body(): pl.pallas_call(functools.partial(kernel, sizes), out_shape=(jax.ShapeDtyp...  37 us
    unnamed x17, local copies, waits for them, and re-layouts  5.95 us
    pallas_call x4, local copies, waits for them, and re-layouts, body(): pl.pallas_call(functools.partial(kernel, sizes), out_shape=(jax.ShapeDtyp...  2.76 us

profile of v1, /device:TPU:0, one launch (start us, length us, event | category | flops | bytes accessed | tf_op | source)
XLA Modules:
  0.0 48.3 jit_solution(17629236522523755173)
XLA Ops:
  0.6 0.0 copy-start.4
  0.6 0.7 %convert_element_type.14 = f32[2,48]{1,0:T(2,128)S(1)} convert(s32[2,48]{1,0:T(2,128)} %param.13) | non-fusion elementwise | flops 96 | bytes 768 | tf_op jit(solution)/shard_map/convert_element_type | solution.py:523
  1.4 0.7 %convert_element_type.15 = f32[2,48]{1,0:T(2,128)S(1)} convert(s32[2,48]{1,0:T(2,128)} %param.14) | non-fusion elementwise | flops 96 | bytes 768 | tf_op jit(solution)/shard_map/convert_element_type | solution.py:524
  2.1 0.8 %copy.22 = f32[40,32]{1,0:T(8,128)S(1)} copy(f32[40,32]{0,1:T(8,128)} %param.17) | data formatting | bytes 10240 | tf_op args[5]
  2.9 0.8 %copy.24 = f32[40,32]{1,0:T(8,128)S(1)} copy(f32[40,32]{0,1:T(8,128)} %param.18) | data formatting | bytes 10240 | tf_op args[6]
  3.7 0.8 %copy.21 = f32[40,20]{1,0:T(8,128)S(1)} copy(f32[40,20]{0,1:T(8,128)} %param.22) | data formatting | bytes 6400 | tf_op args[10]
  4.4 0.1 pad_add_fusion.cw
  4.5 0.1 reshape.27
  4.6 0.1 reshape.26
  4.8 0.8 %copy.17 = f32[2,48,20]{2,1,0:T(8,128)S(1)} copy(f32[2,48,20]{1,0,2:T(2,128)} %param.15) | data formatting | bytes 15360 | tf_op args[3]
  5.6 0.8 %copy.18 = f32[2,48,20]{2,1,0:T(8,128)S(1)} copy(f32[2,48,20]{1,0,2:T(2,128)} %param.16) | data formatting | bytes 15360 | tf_op args[4]
  6.4 0.0 copy-start.2
  6.4 0.1 concatenate.6
  6.6 0.0 copy-done.4
  6.6 0.0 copy-start
  6.6 0.0 copy-start.1
  6.6 0.0 copy-start.3
  6.6 0.3 copy.25.out_map
  6.9 0.4 copy-done.2
  7.4 0.3 copy-done
  7.7 0.2 copy-done.1
  7.8 0.0 copy-done.3
  7.8 37.0 %shard_map.155 = (f32[2,48,576]{2,1,0:T(8,128)S(1)}, f32[2,48,20]{2,1,0:T(8,128)S(1)}, f32[2,48,20]{2,1,0:T(8,128)S(1)}, f32[2,48,20]{2,1,0:T(8,128)S(1)}, f32[2,48,20]{2,1,0:T(8,128)S(1)}) custom-call(f32[2,48,576]{2,1,0:T(8,128)S(1)} %copy-done.2, f32[136,128]{1,0:T(8,128)S(1)} %select_maximum_fusion.pack, f32[8,576]{1,0:T(8,128)S(1)} %copy-done.3, ...), custom_call_target="tpu_custom_call" | custom-call | tf_op jit(solution)/shard_map/pallas_call | solution.py:547
  44.8 0.7 %copy.26 = f32[2,48,20]{1,0,2:T(2,128)} copy(f32[2,48,20]{2,1,0:T(8,128)S(1)} %get-tuple-element.6) | data formatting | bytes 15360 | tf_op jit(solution)/shard_map/pallas_call | solution.py:547
  45.5 0.7 %copy.27 = f32[2,48,20]{1,0,2:T(2,128)} copy(f32[2,48,20]{2,1,0:T(8,128)S(1)} %get-tuple-element.7) | data formatting | bytes 15360 | tf_op jit(solution)/shard_map/pallas_call | solution.py:547
  46.2 0.7 %copy.28 = f32[2,48,20]{1,0,2:T(2,128)} copy(f32[2,48,20]{2,1,0:T(8,128)S(1)} %get-tuple-element.8) | data formatting | bytes 15360 | tf_op jit(solution)/shard_map/pallas_call | solution.py:547
  46.9 0.7 %copy.29 = f32[2,48,20]{1,0,2:T(2,128)} copy(f32[2,48,20]{2,1,0:T(8,128)S(1)} %get-tuple-element.9) | data formatting | bytes 15360 | tf_op jit(solution)/shard_map/pallas_call | solution.py:547
  47.6 0.7 %copy.31 = f32[2,48,576]{2,1,0:T(8,128)} copy(f32[2,48,576]{2,1,0:T(8,128)S(1)} %get-tuple-element.15) | data formatting | bytes 442368
  (3 shorter events, 0.0 us)
Async XLA Ops:
  0.6 5.9 %copy-start.4 = (bf16[512,576]{0,1:T(8,128)(2,1)S(1)}, bf16[512,576]{0,1:T(8,128)(2,1)}, u32[]{:S(2)}) copy-start(bf16[512,576]{0,1:T(8,128)(2,1)} %param.21) | copy-start | bytes 1769476
  6.4 0.9 %copy-start.2 = (f32[2,48,576]{2,1,0:T(8,128)S(1)}, f32[2,48,576]{2,1,0:T(8,128)}, u32[]{:S(2)}) copy-start(f32[2,48,576]{2,1,0:T(8,128)} %spectrum.1) | copy-start | bytes 663556
  6.6 1.1 %copy-start = (bf16[576,512]{1,0:T(8,128)(2,1)S(1)}, bf16[576,512]{1,0:T(8,128)(2,1)}, u32[]{:S(2)}) copy-start(bf16[576,512]{1,0:T(8,128)(2,1)} %left.1) | copy-start | bytes 1769476
  6.6 1.3 %copy-start.1 = (bf16[576,512]{1,0:T(8,128)(2,1)S(1)}, bf16[576,512]{1,0:T(8,128)(2,1)}, u32[]{:S(2)}) copy-start(bf16[576,512]{1,0:T(8,128)(2,1)} %right.1) | copy-start | bytes 1769476
  6.6 1.3 %copy-start.3 = (f32[8,576]{1,0:T(8,128)S(1)}, f32[8,576]{1,0:T(8,128)}, u32[]{:S(2)}) copy-start(f32[8,576]{1,0:T(8,128)} %constant.6.clone.angles) | copy-start | bytes 55300

commit v2 on v1

--- a/solution.py
+++ b/solution.py
@@ -27,6 +27,12 @@
     return jnp.dot(a, b, precision=highest, preferred_element_type=jnp.float32)
 
 
+def dot_on(a, b, dim_a, dim_b, precision=highest):
+    return lax.dot_general(
+        a, b, (((dim_a,), (dim_b,)), ((), ())), precision=precision, preferred_element_type=jnp.float32
+    )
+
+
 def sweep(centre, back_one, back_two, next_one, next_two, velocity):
     up = velocity >= 0.0
     one = jnp.where(up, back_one, next_one)
@@ -65,19 +71,30 @@
 
 def kernel(
     sizes,
-    spectrum,
-    pack,
+    spectrum_hbm,
+    wet_mask,
+    ocean_source,
+    ocean_u,
+    ocean_v,
     angles,
     cw,
     dw,
-    left,
-    right,
-    out_map,
+    left_hbm,
+    right_hbm,
+    out_hbm,
+    mixing,
     spec_out,
     u_out,
     v_out,
     du_out,
     dv_out,
+    spectrum,
+    left,
+    right,
+    out_map,
+    load_sem,
+    pack,
+    currents,
     masked,
     packs,
     own_flow,
@@ -111,9 +128,17 @@
     sea_recv,
 ):
     nx, ny = sizes
+    loads = [
+        pltpu.make_async_copy(src, dst, load_sem.at[k])
+        for k, (src, dst) in enumerate(
+            ((spectrum_hbm, spectrum), (left_hbm, left), (right_hbm, right), (out_hbm, out_map))
+        )
+    ]
+    for load in loads:
+        load.start()
     tile_x, tile_y, bins = spectrum.shape
     half = tile_y // 2
-    own = u_out.shape[2]
+    own = u_out.shape[0]
     rows = 2 * tile_x
     g, gx, gy = lax.axis_index("grp"), lax.axis_index("gx"), lax.axis_index("gy")
     z, y = gx // 2, gx % 2
@@ -156,8 +181,22 @@
             total = total + jnp.where(cond, 1, 0)
 
     columns = tile_x * tile_y
-    wet_n = pack[0:columns, 2 * own : 2 * own + 1]
-    masked[...] = (spectrum[...].reshape(columns, bins) * wet_n).reshape(tile_x, tile_y, bins)
+
+    def as_columns(table):
+        ones = jnp.ones((1, LANES), jnp.float32)
+        values = table[...].astype(jnp.float32)
+        return jnp.concatenate([dot_on(values[r : r + 1], ones, 0, 0) for r in range(tile_x)], axis=0)
+
+    place_i, place_j = iota((own, LANES), 0), iota((own, LANES), 1)
+    place_u = jnp.where(place_j == place_i + own * g, 1.0, 0.0)
+    place_v = jnp.where(place_j == place_i + own * g + NLEV, 1.0, 0.0)
+    for r in range(tile_x):
+        pack[r * tile_y : (r + 1) * tile_y] = dot_on(ocean_u[:, r, :], place_u, 0, 0) + dot_on(
+            ocean_v[:, r, :], place_v, 0, 0
+        )
+    pack[columns:] = dot_on(mixing[...], place_u, 0, 0)
+    wet_wide = as_columns(wet_mask)
+    wet_n = wet_wide[:, 0:1]
 
     @pl.when(z == 0)
     def _():
@@ -194,6 +233,8 @@
 
     to_grp = Move(pack, packs, init_send.at[0], init_recv.at[0], at(1), True, True)
     to_grp.start()
+    loads[0].wait()
+    masked[...] = (spectrum[...].reshape(columns, bins) * wet_n).reshape(tile_x, tile_y, bins)
     away = pl.ds(pl.multiple_of(half * (1 - y), 8), half)
     mine = pl.ds(pl.multiple_of(half * y, 8), half)
     my_rows = pl.ds(tile_x * y, tile_x)
@@ -203,21 +244,18 @@
     to_pair.start()
     field[my_rows] = masked[:, mine, :]
 
-    place_i, place_j = iota((LANES, LANES), 0), iota((LANES, LANES), 1)
-
-    def placing(group):
-        shift = own * group + jnp.where(place_i < own, 0, own)
-        keep = (place_i < 2 * own) & (place_j == place_i + shift)
-        return jnp.where(keep, 1.0, 0.0)
-
+    chosen_at = as_columns(ocean_source)[:, 0:1]
+    chosen = jnp.where(iota((columns, columns), 1).astype(jnp.float32) == chosen_at, 1.0, 0.0)
+    currents[...] = jnp.zeros_like(currents)
+    currents[0:NF, 0:NLEV] = cw[...]
+    currents[NF : 2 * NF] = pltpu.roll(currents[0:NF], NLEV, 1)
     to_grp.wait_recv()
-    everything = exact_dot(pack[...], placing(g)) + exact_dot(packs[...], placing(1 - g))
+    everything = pack[...] + packs[...]
     ocean[...] = everything[:columns].reshape(ocean.shape)
     mix[...] = jnp.zeros_like(mix)
     mix[0:NLEV] = everything[columns:]
     mix[NLEV : 2 * NLEV] = pltpu.roll(everything[columns:], NLEV, 1)
-    chosen = jnp.where(iota((columns, columns), 1).astype(jnp.float32) == pack[0:columns, 2 * own + 1 : 2 * own + 2], 1.0, 0.0)
-    felt = exact_dot(chosen, exact_dot(everything[:columns], cw[...]))
+    felt = exact_dot(chosen, dot_on(everything[:columns], currents[...], 1, 1))
     felt = felt + jnp.where(iota((columns, LANES), 1) == 2 * NF, wet_n, 0.0)
     own_flow[...] = felt.reshape(own_flow.shape)
     flow_pair = Move(
@@ -309,7 +347,7 @@
         product = jnp.dot(now, left[...], preferred_element_type=jnp.float32) * jnp.dot(
             now, right[...], preferred_element_type=jnp.float32
         )
-        result = jnp.dot(product.astype(jnp.bfloat16), out_map[...], preferred_element_type=jnp.float32)
+        result = dot_on(product.astype(jnp.bfloat16), out_map[...], 1, 1, None)
         source[...] = (inter_step * result).reshape(source.shape)
 
     def finish(s, moves):
@@ -397,6 +435,8 @@
     speed_x[...] = (group_speed * cosine + fx).reshape(speed_x.shape)
     speed_y[...] = (group_speed * sine + fy).reshape(speed_x.shape)
     turn[...] = (turning * (sine * fx - cosine * fy)).reshape(speed_x.shape)
+    for load in loads[1:]:
+        load.wait()
     interaction()
     for m in edges_flow:
         m.wait_recv()
@@ -419,7 +459,7 @@
     back = Move(
         field.at[their_rows], spec_out.at[:, mine, :], init_send.at[5], init_recv.at[5], at(0, pair), True, True
     )
-    depth = exact_dot(dw[...], spread_x)
+    depth = dot_on(dw[...], spread_x[0:NF], 0, 0)
     unused = jnp.zeros((LANES - 2 * NLEV, bins), jnp.float32)
     profile = jnp.concatenate([depth * cosine, depth * sine, unused], axis=0)
     drift = lax.dot_general(
@@ -489,18 +529,31 @@
         i, j = iota((LANES, own), 0), iota((LANES, own), 1)
         return jnp.where(i == j + own * g + offset, 1.0, 0.0)
 
-    shape = u_out.shape
     pick_u, pick_v = picking(0), picking(NLEV)
-    du_out[...] = exact_dot(drift_all, pick_u).reshape(shape)
-    dv_out[...] = exact_dot(drift_all, pick_v).reshape(shape)
+
+    def give(out, pick, values):
+        for r in range(tile_x):
+            out[:, r, :] = dot_on(pick, values[r * tile_y : (r + 1) * tile_y], 0, 1)
+
+    give(du_out, pick_u, drift_all)
+    give(dv_out, pick_v, drift_all)
     for m in sea_second:
         m.wait_recv()
     final = ocean_section(ocean_next, neighbours(1, ocean_next), drift_all)
-    u_out[...] = exact_dot(final, pick_u).reshape(shape)
-    v_out[...] = exact_dot(final, pick_v).reshape(shape)
+    give(u_out, pick_u, final)
+    give(v_out, pick_v, final)
     back.wait_recv()
     for m in [to_grp, to_pair, flow_pair, back] + edges_flow + drift_moves + sea_first + sea_second:
         m.wait_send()
+
+
+def store_kernel(*refs):
+    count = (len(refs) - 1) // 2
+    copies = [pltpu.make_async_copy(refs[i], refs[count + i], refs[-1].at[i]) for i in range(count)]
+    for copy in copies:
+        copy.start()
+    for copy in copies:
+        copy.wait()
 
 
 def solution(mesh):
@@ -516,22 +569,6 @@
         own = ocean_u.shape[2]
         columns = tile_x * tile_y
         f32 = jnp.float32
-        pack = jnp.concatenate(
-            [
-                ocean_u.reshape(columns, own),
-                ocean_v.reshape(columns, own),
-                wet_mask.astype(f32).reshape(columns, 1),
-                ocean_source.astype(f32).reshape(columns, 1),
-                jnp.zeros((columns, LANES - 2 * own - 2), f32),
-            ],
-            axis=1,
-        )
-        pack = jnp.concatenate([pack, jnp.pad(mixing, ((0, 0), (0, LANES - own)))], axis=0)
-        low = NLEV
-        cw = jnp.pad(current_weights, ((0, LANES - low), (0, LANES - NF))) + jnp.pad(
-            current_weights, ((low, LANES - 2 * low), (NF, LANES - 2 * NF))
-        )
-        dw = jnp.pad(drift_weights, ((0, 64 - low), (0, LANES - NF)))[:low]
         vmem = pl.BlockSpec(memory_space=pltpu.VMEM)
         sea = (tile_x, tile_y, LANES)
         sections = WAVE_SECTIONS
@@ -543,13 +580,23 @@
         def D(*shape):
             return pltpu.SemaphoreType.DMA(shape)
 
-        small = jax.ShapeDtypeStruct(ocean_u.shape, f32)
-        return pl.pallas_call(
+        outs = (jax.ShapeDtypeStruct(spectrum.shape, f32),) + (
+            jax.ShapeDtypeStruct((own, tile_x, tile_y), f32),
+        ) * 4
+        anywhere = pl.BlockSpec(memory_space=pl.ANY)
+        results = pl.pallas_call(
             functools.partial(kernel, sizes),
-            out_shape=(jax.ShapeDtypeStruct(spectrum.shape, f32), small, small, small, small),
-            in_specs=[vmem] * 8,
+            out_shape=outs,
+            in_specs=[anywhere] + [vmem] * 7 + [anywhere] * 3 + [vmem],
             out_specs=(vmem,) * 5,
             scratch_shapes=[
+                V(tile_x, tile_y, bins),
+                pltpu.VMEM(inter_left.shape, inter_left.dtype),
+                pltpu.VMEM(inter_right.shape, inter_right.dtype),
+                pltpu.VMEM(inter_out.shape[::-1], inter_out.dtype),
+                D(4),
+                V(columns + NLEV, LANES),
+                V(LANES, LANES),
                 V(tile_x, tile_y, bins),
                 V(columns + NLEV, LANES),
                 V(*sea),
@@ -582,8 +629,29 @@
                 D(2, 4),
                 D(2, 4),
             ],
-            compiler_params=pltpu.CompilerParams(collective_id=0, has_side_effects=True, vmem_limit_bytes=40 * 2**20),
-        )(spectrum, pack, jnp.asarray(table), cw, dw, inter_left, inter_right, inter_out)
+            compiler_params=pltpu.CompilerParams(collective_id=0, has_side_effects=True),
+        )(
+            spectrum,
+            wet_mask,
+            ocean_source,
+            jnp.transpose(ocean_u, (2, 0, 1)),
+            jnp.transpose(ocean_v, (2, 0, 1)),
+            jnp.asarray(table),
+            current_weights.T,
+            drift_weights.T,
+            inter_left,
+            inter_right,
+            inter_out.T,
+            mixing.T,
+        )
+        results = pl.pallas_call(
+            store_kernel,
+            out_shape=outs,
+            in_specs=[vmem] * 5,
+            out_specs=(anywhere,) * 5,
+            scratch_shapes=[D(5)],
+        )(*results)
+        return (results[0],) + tuple(jnp.transpose(a, (1, 2, 0)) for a in results[1:])
 
     tile = P("gx", "gy", "grp")
     in_specs = (

time: 48.7 us -> 41.4 us (0.85)
  local copies, waits for them, and re-layouts: 9.07 us -> 0 us
  Pallas kernels: 37 us -> 40.5 us
  other arithmetic: 1.51 us -> 0 us
    unnamed x17 -> x0, local copies, waits for them, and re-layouts: 5.95 us -> none
    pallas_call x1 -> x2, Pallas kernels: 37 us -> 40.5 us  [the longest x1 38.8 us: body(): pl.pallas_call(functools.partial(kernel, sizes), out_shape=outs, in_specs...]
    pallas_call x4 -> x0, local copies, waits for them, and re-layouts: 2.76 us -> none  [body(): pl.pallas_call(functools.partial(kernel, sizes), out_shape=(jax.ShapeDtyp...]
    convert_element_type x2 -> x0, other arithmetic: 1.42 us -> none  [the longest x1 0.74 us: body(): wet_mask.astype(f32).reshape(columns, 1)]
where the time goes in v2:
time: 41.4 us; the launch traced here: 41.2 us
  Pallas kernels  40.5 us (98%)
  between operations  0.64 us (2%)
    pallas_call x1, Pallas kernels, body(): pl.pallas_call(functools.partial(kernel, sizes), out_shape=outs, in_specs...  38.8 us
    pallas_call x1, Pallas kernels, body(): pl.pallas_call(store_kernel, out_shape=outs, in_specs=[vmem] * 5, out_spe...  1.73 us

profile of v2, /device:TPU:0, one launch (start us, length us, event | category | flops | bytes accessed | tf_op | source)
XLA Modules:
  0.0 41.2 jit_solution(1179058781154721219)
XLA Ops:
  0.6 38.8 %shard_map.155 = (f32[2,48,576]{2,1,0:T(8,128)}, f32[20,2,48]{2,1,0:T(2,128)}, f32[20,2,48]{2,1,0:T(2,128)}, f32[20,2,48]{2,1,0:T(2,128)}, f32[20,2,48]{2,1,0:T(2,128)}) custom-call(f32[2,48,576]{2,1,0:T(8,128)} %spectrum_hbm.1, s32[2,48]{1,0:T(2,128)} %wet_mask.1, s32[2,48]{1,0:T(2,128)} %ocean_source.1, f32[20,2,48]{2,1,0:T(2,128)} %bitcast.11, ...), custom_call_target="tpu_custom_call" | custom-call | tf_op jit(solution)/shard_map/pallas_call | solution.py:587
  39.4 1.7 %shard_map.156 = (f32[2,48,576]{2,1,0:T(8,128)}, f32[20,2,48]{2,1,0:T(2,128)}, f32[20,2,48]{2,1,0:T(2,128)}, f32[20,2,48]{2,1,0:T(2,128)}, f32[20,2,48]{2,1,0:T(2,128)}) custom-call(f32[2,48,576]{2,1,0:T(8,128)} %get-tuple-element.15.refs_0_, f32[20,2,48]{2,1,0:T(2,128)} %get-tuple-element.16.refs_1_, f32[20,2,48]{2,1,0:T(2,128)} %get-tuple-element.17.refs_2_, ...), custom_call_target="tpu_custom_call" | custom-call | tf_op jit(solution)/shard_map/pallas_call | solution.py:647

commit v3 on v2

--- a/solution.py
+++ b/solution.py
@@ -229,12 +229,13 @@
         def _():
             col_halo[:, side] = jnp.zeros_like(col_halo[:, side])
 
+    loads[0].wait()
+    masked[...] = (spectrum[...].reshape(columns, bins) * wet_n).reshape(tile_x, tile_y, bins)
+
     pl.semaphore_wait(barrier, total)
 
     to_grp = Move(pack, packs, init_send.at[0], init_recv.at[0], at(1), True, True)
     to_grp.start()
-    loads[0].wait()
-    masked[...] = (spectrum[...].reshape(columns, bins) * wet_n).reshape(tile_x, tile_y, bins)
     away = pl.ds(pl.multiple_of(half * (1 - y), 8), half)
     mine = pl.ds(pl.multiple_of(half * y, 8), half)
     my_rows = pl.ds(tile_x * y, tile_x)
@@ -243,68 +244,6 @@
     )
     to_pair.start()
     field[my_rows] = masked[:, mine, :]
-
-    chosen_at = as_columns(ocean_source)[:, 0:1]
-    chosen = jnp.where(iota((columns, columns), 1).astype(jnp.float32) == chosen_at, 1.0, 0.0)
-    currents[...] = jnp.zeros_like(currents)
-    currents[0:NF, 0:NLEV] = cw[...]
-    currents[NF : 2 * NF] = pltpu.roll(currents[0:NF], NLEV, 1)
-    to_grp.wait_recv()
-    everything = pack[...] + packs[...]
-    ocean[...] = everything[:columns].reshape(ocean.shape)
-    mix[...] = jnp.zeros_like(mix)
-    mix[0:NLEV] = everything[columns:]
-    mix[NLEV : 2 * NLEV] = pltpu.roll(everything[columns:], NLEV, 1)
-    felt = exact_dot(chosen, dot_on(everything[:columns], currents[...], 1, 1))
-    felt = felt + jnp.where(iota((columns, LANES), 1) == 2 * NF, wet_n, 0.0)
-    own_flow[...] = felt.reshape(own_flow.shape)
-    flow_pair = Move(
-        own_flow.at[:, away, :], flow.at[my_rows], init_send.at[2], init_recv.at[2], at(0, pair), True, True
-    )
-    flow_pair.start()
-    flow[my_rows] = own_flow[:, mine, :]
-
-    def sea_moves(k, array):
-        moves = []
-        for side, d in ((0, -1), (1, 1)):
-            moves.append(
-                Move(
-                    array.at[0 if d < 0 else tile_x - 1],
-                    row_halo.at[k, 1 - side],
-                    sea_send.at[k, side],
-                    sea_recv.at[k, side],
-                    at(0, gx + d),
-                    inside(gx, d, nx),
-                    inside(gx, -d, nx),
-                )
-            )
-            moves.append(
-                Move(
-                    col_edge.at[k, side],
-                    col_halo.at[k, 1 - side],
-                    sea_send.at[k, 2 + side],
-                    sea_recv.at[k, 2 + side],
-                    at(0, gx, gy + d),
-                    inside(gy, d, ny),
-                    inside(gy, -d, ny),
-                )
-            )
-        return moves
-
-    def set_col_edges(k, array):
-        for side, column in ((0, 0), (1, tile_y - 1)):
-            for r in range(tile_x):
-                col_edge[k, side, r : r + 1, :] = array[r, column : column + 1, :]
-
-    lane = iota((1, bins), 1)
-    frequency = (g * NFL + (lane & (NFL - 1))).astype(jnp.float32)
-    group_speed = 0.2 + 0.4 * (NF - 1 - frequency) / (NF - 1)
-    turning = 0.5 * (frequency + 1.0) / NF
-    cosine, sine = angles[0:1, :], angles[1:2, :]
-    spread_i = iota((LANES, bins), 0)
-    spread_f = g * NFL + (iota((LANES, bins), 1) & (NFL - 1))
-    spread_x = jnp.where(spread_i == spread_f, 1.0, 0.0)
-    spread_y = jnp.where(spread_i == spread_f + NF, 1.0, 0.0)
 
     def wave_moves(s):
         moves = []
@@ -337,6 +276,72 @@
                 k += 1
         return moves
 
+    first_moves = wave_moves(0)
+    pl.when(y == 0)(first_moves[0].start)
+    pl.when(y == 1)(first_moves[1].start)
+
+    chosen_at = as_columns(ocean_source)[:, 0:1]
+    chosen = jnp.where(iota((columns, columns), 1).astype(jnp.float32) == chosen_at, 1.0, 0.0)
+    currents[...] = jnp.zeros_like(currents)
+    currents[0:NF, 0:NLEV] = cw[...]
+    currents[NF : 2 * NF] = pltpu.roll(currents[0:NF], NLEV, 1)
+    to_grp.wait_recv()
+    everything = pack[...] + packs[...]
+    ocean[...] = everything[:columns].reshape(ocean.shape)
+    mix[...] = jnp.zeros_like(mix)
+    mix[0:NLEV] = everything[columns:]
+    mix[NLEV : 2 * NLEV] = pltpu.roll(everything[columns:], NLEV, 1)
+    felt = exact_dot(chosen, dot_on(everything[:columns], currents[...], 1, 1))
+    felt = felt + jnp.where(iota((columns, LANES), 1) == 2 * NF, wet_n, 0.0)
+    own_flow[...] = felt.reshape(own_flow.shape)
+    flow_pair = Move(
+        own_flow.at[:, away, :], flow.at[my_rows], init_send.at[2], init_recv.at[2], at(0, pair), True, True
+    )
+    flow_pair.start()
+    flow[my_rows] = own_flow[:, mine, :]
+
+    def sea_moves(k, array):
+        moves = []
+        for side, d in ((0, -1), (1, 1)):
+            moves.append(
+                Move(
+                    array.at[0 if d < 0 else tile_x - 1],
+                    row_halo.at[k, 1 - side],
+                    sea_send.at[k, side],
+                    sea_recv.at[k, side],
+                    at(0, gx + d),
+                    inside(gx, d, nx),
+                    inside(gx, -d, nx),
+                )
+            )
+            moves.append(
+                Move(
+                    col_edge.at[k, side],
+                    col_halo.at[k, 1 - side],
+                    sea_send.at[k, 2 + side],
+                    sea_recv.at[k, 2 + side],
+                    at(0, gx, gy + d),
+                    inside(gy, d, ny),
+                    inside(gy, -d, ny),
+                )
+            )
+        return moves
+
+    def set_col_edges(k, array):
+        for side, column in ((0, 0), (1, tile_y - 1)):
+            for r in range(tile_x):
+                col_edge[k, side, r : r + 1, :] = array[r, column : column + 1, :]
+
+    lane = iota((1, bins), 1)
+    frequency = (g * NFL + (lane & (NFL - 1))).astype(jnp.float32)
+    group_speed = 0.2 + 0.4 * (NF - 1 - frequency) / (NF - 1)
+    turning = 0.5 * (frequency + 1.0) / NF
+    cosine, sine = angles[0:1, :], angles[1:2, :]
+    spread_i = iota((LANES, bins), 0)
+    spread_f = g * NFL + (iota((LANES, bins), 1) & (NFL - 1))
+    spread_x = jnp.where(spread_i == spread_f, 1.0, 0.0)
+    spread_y = jnp.where(spread_i == spread_f + NF, 1.0, 0.0)
+
     def set_edges(s):
         for side, first in ((0, 0), (1, half - 2)):
             for r in range(rows):
@@ -415,9 +420,10 @@
 
     to_pair.wait_recv()
     set_edges(0)
-    first_moves = wave_moves(0)
-    for m in first_moves:
+    for m in first_moves[2:]:
         m.start()
+    pl.when(y == 1)(first_moves[0].start)
+    pl.when(y == 0)(first_moves[1].start)
     set_col_edges(0, ocean)
     flow_pair.wait_recv()
     for side, first in ((0, 0), (1, half - 2)):
@@ -447,7 +453,7 @@
     def section(s, carry):
         set_edges(s)
         moves = wave_moves(s)
-        for m in moves:
+        for m in moves[2:] + moves[:2]:
             m.start()
         interaction()
         finish(s, moves)
@@ -586,7 +592,7 @@
         anywhere = pl.BlockSpec(memory_space=pl.ANY)
         results = pl.pallas_call(
             functools.partial(kernel, sizes),
-            out_shape=outs,
+            out_shape=tuple(pltpu.VMEM(a.shape, a.dtype) for a in outs),
             in_specs=[anywhere] + [vmem] * 7 + [anywhere] * 3 + [vmem],
             out_specs=(vmem,) * 5,
             scratch_shapes=[
@@ -647,10 +653,10 @@
         results = pl.pallas_call(
             store_kernel,
             out_shape=outs,
-            in_specs=[vmem] * 5,
+            in_specs=[anywhere] * 5,
             out_specs=(anywhere,) * 5,
             scratch_shapes=[D(5)],
-        )(*results)
+        )(*(pltpu.with_memory_space_constraint(a, pltpu.VMEM) for a in results))
         return (results[0],) + tuple(jnp.transpose(a, (1, 2, 0)) for a in results[1:])
 
     tile = P("gx", "gy", "grp")

time: 41.4 us -> 39.4 us (0.952)
  Pallas kernels: 40.5 us -> 38.5 us
    pallas_call x2, Pallas kernels: 40.5 us -> 38.5 us  [the longest x1 37.8 us: body(): pl.pallas_call(functools.partial(kernel, sizes), out_shape=tuple((pltpu.V...]
where the time goes in v3:
time: 39.4 us; the launch traced here: 39.1 us
  Pallas kernels  38.5 us (98%)
  between operations  0.64 us (2%)
    pallas_call x1, Pallas kernels, body(): pl.pallas_call(functools.partial(kernel, sizes), out_shape=tuple((pltpu.V...  37.8 us

profile of v3, /device:TPU:0, one launch (start us, length us, event | category | flops | bytes accessed | tf_op | source)
XLA Modules:
  0.0 39.1 jit_solution(10419481246065756505)
XLA Ops:
  0.6 37.8 %shard_map.155 = (f32[2,48,576]{2,1,0:T(8,128)S(1)}, f32[20,2,48]{2,1,0:T(2,128)S(1)}, f32[20,2,48]{2,1,0:T(2,128)S(1)}, f32[20,2,48]{2,1,0:T(2,128)S(1)}, f32[20,2,48]{2,1,0:T(2,128)S(1)}) custom-call(f32[2,48,576]{2,1,0:T(8,128)} %spectrum_hbm.1, s32[2,48]{1,0:T(2,128)} %wet_mask.1, s32[2,48]{1,0:T(2,128)} %ocean_source.1, f32[20,2,48]{2,1,0:T(2,128)} %bitcast.11, ...), custom_call_target="tpu_custom_call" | custom-call | tf_op jit(solution)/shard_map/pallas_call | solution.py:593
  38.4 0.8 %shard_map.156 = (f32[2,48,576]{2,1,0:T(8,128)}, f32[20,2,48]{2,1,0:T(2,128)}, f32[20,2,48]{2,1,0:T(2,128)}, f32[20,2,48]{2,1,0:T(2,128)}, f32[20,2,48]{2,1,0:T(2,128)}) custom-call(f32[2,48,576]{2,1,0:T(8,128)S(1)} %get-tuple-element.15.refs_0_, f32[20,2,48]{2,1,0:T(2,128)S(1)} %get-tuple-element.16.refs_1_, f32[20,2,48]{2,1,0:T(2,128)S(1)} %get-tuple-element.17.refs_2_, ...), custom_call_target="tpu_custom_call" | custom-call | tf_op jit(solution)/shard_map/pallas_call | solution.py:653

commit v4 on v3

--- a/solution.py
+++ b/solution.py
@@ -105,6 +105,8 @@
     edge,
     halo_x,
     halo_y,
+    corner,
+    halo_c,
     speed_x,
     speed_y,
     turn,
@@ -211,13 +213,14 @@
         @pl.when(jnp.logical_not(inside(q, dq, nq)))
         def _():
             halo_y[:, side] = jnp.zeros_like(halo_y[:, side])
+            halo_c[:, side] = jnp.zeros_like(halo_c[:, side])
             flow_halo[side] = jnp.zeros_like(flow_halo[side])
 
-        for slot, dz in ((0, -1), (2, 1)):
+        for slot, dz in ((0, -1), (1, 1)):
 
             @pl.when(inside(q, dq, nq) & jnp.logical_not(inside(z, dz, nz)))
             def _():
-                halo_y[:, side, slot] = jnp.zeros_like(halo_y[:, side, slot])
+                halo_c[:, side, slot] = jnp.zeros_like(halo_c[:, side, slot])
 
     for side, d in ((0, -1), (1, 1)):
 
@@ -239,33 +242,45 @@
     away = pl.ds(pl.multiple_of(half * (1 - y), 8), half)
     mine = pl.ds(pl.multiple_of(half * y, 8), half)
     my_rows = pl.ds(tile_x * y, tile_x)
-    to_pair = Move(
-        masked.at[:, away, :], field.at[my_rows], init_send.at[1], init_recv.at[1], at(0, pair), True, True
-    )
-    to_pair.start()
+    to_pair = [
+        Move(
+            masked.at[row, away, :],
+            field.at[tile_x * y + row],
+            init_send.at[k],
+            init_recv.at[k],
+            at(0, pair),
+            True,
+            True,
+        )
+        for k, row in ((1, y), (9, 1 - y))
+    ]
+    for m in to_pair:
+        m.start()
     field[my_rows] = masked[:, mine, :]
 
     def wave_moves(s):
         moves = []
-        for side, dz in ((0, -1), (1, 1)):
-            moves.append(
-                Move(
-                    field.at[pl.ds(0 if dz < 0 else rows - 2, 2)],
-                    halo_x.at[s, 1 - side],
-                    wave_send.at[s, side],
-                    wave_recv.at[s, side],
-                    at(0, gx + 2 * dz),
-                    inside(z, dz, nz),
-                    inside(z, -dz, nz),
+        for near in (True, False):
+            for side, dz in ((0, -1), (1, 1)):
+                layer = 0 if near == (dz < 0) else 1
+                moves.append(
+                    Move(
+                        field.at[layer if dz < 0 else rows - 2 + layer],
+                        halo_x.at[s, 1 - side, layer],
+                        wave_send.at[s, len(moves)],
+                        wave_recv.at[s, len(moves)],
+                        at(0, gx + 2 * dz),
+                        inside(z, dz, nz),
+                        inside(z, -dz, nz),
+                    )
                 )
-            )
-        k = 2
+        k = 4
         for side, dq in ((0, -1), (1, 1)):
             for dz in (-1, 0, 1):
                 moves.append(
                     Move(
-                        edge.at[s, side],
-                        halo_y.at[s, 1 - side, 1 - dz],
+                        edge.at[s, side] if dz == 0 else corner.at[s, side, (1 + dz) // 2],
+                        halo_y.at[s, 1 - side] if dz == 0 else halo_c.at[s, 1 - side, (1 - dz) // 2],
                         wave_send.at[s, k],
                         wave_recv.at[s, k],
                         q_at(dz, dq),
@@ -277,8 +292,9 @@
         return moves
 
     first_moves = wave_moves(0)
-    pl.when(y == 0)(first_moves[0].start)
-    pl.when(y == 1)(first_moves[1].start)
+    for k in (0, 2):
+        pl.when(y == 0)(first_moves[k].start)
+        pl.when(y == 1)(first_moves[k + 1].start)
 
     chosen_at = as_columns(ocean_source)[:, 0:1]
     chosen = jnp.where(iota((columns, columns), 1).astype(jnp.float32) == chosen_at, 1.0, 0.0)
@@ -345,7 +361,9 @@
     def set_edges(s):
         for side, first in ((0, 0), (1, half - 2)):
             for r in range(rows):
-                edge[s, side, 2 * r : 2 * r + 2, :] = field[r, first : first + 2, :]
+                pair_of = field[r, first : first + 2, :]
+                edge[s, side, 2 * r : 2 * r + 2, :] = pair_of
+                corner[s, side, r // 2, 2 * (r % 2) : 2 * (r % 2) + 2, :] = pair_of
 
     def interaction():
         now = field[...].reshape(rows * half, bins).astype(jnp.bfloat16)
@@ -356,10 +374,11 @@
         source[...] = (inter_step * result).reshape(source.shape)
 
     def finish(s, moves):
-        for m in moves:
+        for m in moves[4:]:
             m.wait_recv()
         for side, speed, start in ((0, speed_l, 6), (1, speed_r, half + 8)):
-            before, here, after = (halo_y[s, side, i] for i in range(3))
+            here = halo_y[s, side]
+            before, after = (jnp.concatenate([halo_c[s, side, i]] * 2, axis=0) for i in range(2))
             low = iota((8, bins), 0)
 
             def joined(a, b, n):
@@ -383,13 +402,13 @@
                 return halo_x[s, 1, r - rows]
             return field[r]
 
-        for r in range(rows):
+        waits = {1: moves[0:2], 0: moves[2:4]}
+        for r in [*range(1, rows - 1), 0, rows - 1]:
+            for m in waits.get(r, ()):
+                m.wait_recv()
             wide[r, 8 : 8 + half, :] = sweep(
                 line(r), line(r - 1), line(r - 2), line(r + 1), line(r + 2), speed_x[r]
             )
-        for m in moves:
-            m.wait_send()
-        for r in range(rows):
             b = sweep(
                 wide[r, 8 : 8 + half, :],
                 wide[r, 7 : 7 + half, :],
@@ -402,7 +421,10 @@
             behind = jnp.concatenate([b[:, bins - NFL :], b[:, : bins - NFL]], axis=1)
             ahead = jnp.concatenate([b[:, NFL:], b[:, :NFL]], axis=1)
             c = b - jnp.abs(t) * (b - jnp.where(t >= 0.0, behind, ahead))
-            field[r] = flow[r, :, 2 * NF : 2 * NF + 1] * (c + source[r])
+            source[r] = flow[r, :, 2 * NF : 2 * NF + 1] * (c + source[r])
+        for m in moves:
+            m.wait_send()
+        field[...] = source[...]
 
     def flow_moves():
         return [
@@ -418,12 +440,20 @@
             for side, dq in ((0, -1), (1, 1))
         ]
 
-    to_pair.wait_recv()
-    set_edges(0)
-    for m in first_moves[2:]:
-        m.start()
+    def received(k, row):
+        Move(
+            masked.at[row, away, :], field.at[tile_x * (1 - y) + row], init_send.at[k], init_recv.at[k], at(0, pair), True, True
+        ).wait_recv()
+
+    received(1, 1 - y)
     pl.when(y == 1)(first_moves[0].start)
     pl.when(y == 0)(first_moves[1].start)
+    received(9, y)
+    set_edges(0)
+    for m in first_moves[4:]:
+        m.start()
+    pl.when(y == 1)(first_moves[2].start)
+    pl.when(y == 0)(first_moves[3].start)
     set_col_edges(0, ocean)
     flow_pair.wait_recv()
     for side, first in ((0, 0), (1, half - 2)):
@@ -453,7 +483,7 @@
     def section(s, carry):
         set_edges(s)
         moves = wave_moves(s)
-        for m in moves[2:] + moves[:2]:
+        for m in moves[4:] + moves[:4]:
             m.start()
         interaction()
         finish(s, moves)
@@ -549,7 +579,7 @@
     give(u_out, pick_u, final)
     give(v_out, pick_v, final)
     back.wait_recv()
-    for m in [to_grp, to_pair, flow_pair, back] + edges_flow + drift_moves + sea_first + sea_second:
+    for m in [to_grp, flow_pair, back] + to_pair + edges_flow + drift_moves + sea_first + sea_second:
         m.wait_send()
 
 
@@ -612,7 +642,9 @@
                 V(*wave),
                 V(sections, 2, 8, bins),
                 V(sections, 2, 2, half, bins),
-                V(sections, 2, 3, 8, bins),
+                V(sections, 2, 8, bins),
+                V(sections, 2, 2, 4, bins),
+                V(sections, 2, 2, 4, bins),
                 V(*wave),
                 V(*wave),
                 V(*wave),
@@ -628,10 +660,10 @@
                 V(2, 2, 8, LANES),
                 V(rows, half, LANES),
                 V(2, *sea),
-                D(9),
-                D(9),
-                D(sections, 8),
-                D(sections, 8),
+                D(10),
+                D(10),
+                D(sections, 10),
+                D(sections, 10),
                 D(2, 4),
                 D(2, 4),
             ],

time: 39.4 us -> 38.4 us (0.975)
  Pallas kernels: 38.5 us -> 37.6 us
    pallas_call x1, Pallas kernels: 37.8 us -> 36.8 us  [body(): pl.pallas_call(functools.partial(kernel, sizes), out_shape=tuple((pltpu.V...]
where the time goes in v4:
time: 38.4 us; the launch traced here: 38.2 us
  Pallas kernels  37.6 us (98%)
  between operations  0.64 us (2%)
    pallas_call x1, Pallas kernels, body(): pl.pallas_call(functools.partial(kernel, sizes), out_shape=tuple((pltpu.V...  36.8 us

profile of v4, /device:TPU:0, one launch (start us, length us, event | category | flops | bytes accessed | tf_op | source)
XLA Modules:
  0.0 38.2 jit_solution(16950703167121313360)
XLA Ops:
  0.6 36.8 %shard_map.155 = (f32[2,48,576]{2,1,0:T(8,128)S(1)}, f32[20,2,48]{2,1,0:T(2,128)S(1)}, f32[20,2,48]{2,1,0:T(2,128)S(1)}, f32[20,2,48]{2,1,0:T(2,128)S(1)}, f32[20,2,48]{2,1,0:T(2,128)S(1)}) custom-call(f32[2,48,576]{2,1,0:T(8,128)} %spectrum_hbm.1, s32[2,48]{1,0:T(2,128)} %wet_mask.1, s32[2,48]{1,0:T(2,128)} %ocean_source.1, f32[20,2,48]{2,1,0:T(2,128)} %bitcast.11, ...), custom_call_target="tpu_custom_call" | custom-call | tf_op jit(solution)/shard_map/pallas_call | solution.py:623
  37.5 0.8 %shard_map.156 = (f32[2,48,576]{2,1,0:T(8,128)}, f32[20,2,48]{2,1,0:T(2,128)}, f32[20,2,48]{2,1,0:T(2,128)}, f32[20,2,48]{2,1,0:T(2,128)}, f32[20,2,48]{2,1,0:T(2,128)}) custom-call(f32[2,48,576]{2,1,0:T(8,128)S(1)} %get-tuple-element.15.refs_0_, f32[20,2,48]{2,1,0:T(2,128)S(1)} %get-tuple-element.16.refs_1_, f32[20,2,48]{2,1,0:T(2,128)S(1)} %get-tuple-element.17.refs_2_, ...), custom_call_target="tpu_custom_call" | custom-call | tf_op jit(solution)/shard_map/pallas_call | solution.py:685

commit v5 on v4

--- a/solution.py
+++ b/solution.py
@@ -95,6 +95,7 @@
     load_sem,
     pack,
     currents,
+    profile,
     masked,
     packs,
     own_flow,
@@ -474,6 +475,10 @@
     for load in loads[1:]:
         load.wait()
     interaction()
+    depth = dot_on(dw[...], spread_x[0:NF], 0, 0)
+    profile[0:NLEV] = depth * cosine
+    profile[NLEV : 2 * NLEV] = depth * sine
+    profile[2 * NLEV :] = jnp.zeros((LANES - 2 * NLEV, bins), jnp.float32)
     for m in edges_flow:
         m.wait_recv()
     speed_l[...] = group_speed * cosine + exact_dot(flow_halo[0], spread_x)
@@ -495,12 +500,9 @@
     back = Move(
         field.at[their_rows], spec_out.at[:, mine, :], init_send.at[5], init_recv.at[5], at(0, pair), True, True
     )
-    depth = dot_on(dw[...], spread_x[0:NF], 0, 0)
-    unused = jnp.zeros((LANES - 2 * NLEV, bins), jnp.float32)
-    profile = jnp.concatenate([depth * cosine, depth * sine, unused], axis=0)
     drift = lax.dot_general(
         field[...].reshape(rows * half, bins),
-        profile,
+        profile[...],
         (((1,), (1,)), ((), ())),
         precision=highest,
         preferred_element_type=jnp.float32,
@@ -518,8 +520,8 @@
         )
         for k, (yy, device) in enumerate(((y, at(1)), (1 - y, at(1, pair)), (1 - y, at(0, pair))))
     ]
-    for m in drift_moves:
-        m.start()
+    for k in (1, 2, 0):
+        drift_moves[k].start()
     back.start()
     spec_out[:, mine, :] = field[my_rows]
     drift_n[g, :, mine, :] = drift_q[my_rows]
@@ -633,6 +635,7 @@
                 D(4),
                 V(columns + NLEV, LANES),
                 V(LANES, LANES),
+                V(LANES, bins),
                 V(tile_x, tile_y, bins),
                 V(columns + NLEV, LANES),
                 V(*sea),

time: 38.4 us -> 37.9 us (0.987)
  Pallas kernels: 37.6 us -> 37 us
    pallas_call x1, Pallas kernels: 36.8 us -> 36.2 us  [body(): pl.pallas_call(functools.partial(kernel, sizes), out_shape=tuple((pltpu.V...]
where the time goes in v5:
time: 37.9 us; the launch traced here: 37.6 us
  Pallas kernels  37 us (98%)
  between operations  0.64 us (2%)
    pallas_call x1, Pallas kernels, body(): pl.pallas_call(functools.partial(kernel, sizes), out_shape=tuple((pltpu.V...  36.2 us

profile of v5, /device:TPU:0, one launch (start us, length us, event | category | flops | bytes accessed | tf_op | source)
XLA Modules:
  0.0 37.6 jit_solution(15744491013106855845)
XLA Ops:
  0.6 36.2 %shard_map.155 = (f32[2,48,576]{2,1,0:T(8,128)S(1)}, f32[20,2,48]{2,1,0:T(2,128)S(1)}, f32[20,2,48]{2,1,0:T(2,128)S(1)}, f32[20,2,48]{2,1,0:T(2,128)S(1)}, f32[20,2,48]{2,1,0:T(2,128)S(1)}) custom-call(f32[2,48,576]{2,1,0:T(8,128)} %spectrum_hbm.1, s32[2,48]{1,0:T(2,128)} %wet_mask.1, s32[2,48]{1,0:T(2,128)} %ocean_source.1, f32[20,2,48]{2,1,0:T(2,128)} %bitcast.11, ...), custom_call_target="tpu_custom_call" | custom-call | tf_op jit(solution)/shard_map/pallas_call | solution.py:625
  36.9 0.8 %shard_map.156 = (f32[2,48,576]{2,1,0:T(8,128)}, f32[20,2,48]{2,1,0:T(2,128)}, f32[20,2,48]{2,1,0:T(2,128)}, f32[20,2,48]{2,1,0:T(2,128)}, f32[20,2,48]{2,1,0:T(2,128)}) custom-call(f32[2,48,576]{2,1,0:T(8,128)S(1)} %get-tuple-element.15.refs_0_, f32[20,2,48]{2,1,0:T(2,128)S(1)} %get-tuple-element.16.refs_1_, f32[20,2,48]{2,1,0:T(2,128)S(1)} %get-tuple-element.17.refs_2_, ...), custom_call_target="tpu_custom_call" | custom-call | tf_op jit(solution)/shard_map/pallas_call | solution.py:688
